TPU v7x, 32 devices: a whole 2x2x4 slice. The times are simulated.
32 devices in a mesh: groups: 2 (over y), dp: 4 (over z), col: 4 (over x, core).
Axes of the slice: x: 2, y: 2, z: 4, core: 2. Of those that a mesh axis runs over, the one named last changes fastest.
Arguments:
- points: float32 [16384, 256], P(('groups', 'dp')), parts along dimension 0, may hold values from -10 to 10
- point_ids: int32 [16384], P(('groups', 'dp')), parts along dimension 0, may hold values from 0 to 8191, as said below
- landmark_ids: int32 [2048], P(('groups', 'col')), parts along dimension 0, may hold values from 0 to 8191, as said below
Outputs:
- factor: float32 [2048, 1024], P('groups', 'col'), parts along dimension 0
There are 2 independent parts, one for each index of `groups`. A program takes and returns all parts, laid end to end along the dimension named above; each array names one. Nothing has to cross between parts.
Inputs may be any that keep to these rules, and one draw needn't show every extreme that they name: `point_ids`: a permutation of the numbers 0 to 8191. `landmark_ids`: 1024 distinct ids, each the id of some point; the indices of dp that hold these points hold unequal numbers of them.
All inputs are finite; a program needn't handle non-finite values.
Results may differ from a plain program's by a relative error of at most 0.0003.
Values sent between devices are 32-bit elements; how exact they have to be, the bound alone decides.
No kernel may reach another device: no remote copies, remote signals or barrier semaphores. Data moves between devices by JAX's collectives and lax.ppermute only.
A program may use at most 64 MiB of HBM per device.

v0:
```python
import jax
import jax.numpy as jnp
from jax import lax
from jax.sharding import PartitionSpec as P

LAND = 1024


precise = lax.Precision.HIGHEST


def kernel_panel(points, point_norms, centers):
    center_norms = jnp.sum(centers * centers, axis=1)
    inner = lax.dot_general(
        points,
        centers,
        (((1,), (1,)), ((), ())),
        precision=precise,
        preferred_element_type=jnp.float32,
    )
    distance = point_norms[:, None] + center_norms[None, :] - 2.0 * inner
    return jnp.exp(distance * (-2.0 / points.shape[1]))


def cross_rows(left_panel, right_panel):
    return lax.dot_general(
        left_panel,
        right_panel,
        (((0,), (0,)), ((), ())),
        precision=precise,
        preferred_element_type=jnp.float32,
    )


def local(points, point_ids, landmark_ids):
    land_count = LAND
    land_cols = landmark_ids.shape[0]
    col_count = lax.axis_size("col")
    column_index = lax.axis_index("col")
    matches = (landmark_ids[:, None] == point_ids[None, :]).astype(jnp.float32)
    picked_rows = jnp.dot(matches, points, precision=precise, preferred_element_type=jnp.float32)
    centers = lax.psum(picked_rows, "dp")
    point_norms = jnp.sum(points * points, axis=1)
    own_panel = kernel_panel(points, point_norms, centers)
    product = cross_rows(lax.all_gather(own_panel, "col", axis=1, tiled=True), own_panel)
    gram_part = lax.psum_scatter(product, "dp", scatter_dimension=0, tiled=True)
    dp_count = lax.axis_size("dp")
    gathered = lax.all_gather(gram_part, ("dp", "col"), axis=0, tiled=True)
    gram = gathered.reshape(dp_count, col_count, land_count // dp_count, land_cols)
    gram = gram.transpose(0, 2, 1, 3).reshape(land_count, land_count)
    lower_factor = jnp.linalg.cholesky(gram)
    own_rows = lax.dynamic_slice_in_dim(lower_factor, column_index * land_cols, land_cols, 0)
    return own_rows.T


def solution(mesh):
    in_specs = (P(("groups", "dp"), None), P(("groups", "dp")), P(("groups", "col")))
    out_specs = P("groups", "col")
    return jax.shard_map(local, mesh=mesh, in_specs=in_specs, out_specs=out_specs, check_vma=False)
```

profile of v0, /device:TPU:0, one launch (start us, length us, event | category | flops | bytes accessed | tf_op | source)
XLA Modules:
  0.0 436.7 jit_solution(8690827671123936031)
XLA Ops:
  12.4 36.5 %all-reduce.3.cloned.1.call-done = f32[256,256]{1,0:T(8,128)} async-done(((f32[256,256]{1,0:T(8,128)}), f32[256,256]{1,0:T(8,128)}) %all-reduce.3.cloned.1.call-update) | async-done | bytes 262160 | tf_op jit(solution)/shard_map/psum | solution.py:42
  49.9 4.6 %fusion.4 = f32[2048,256]{0,1:T(8,128)} fusion(f32[256,256]{1,0:T(8,128)} %all-reduce.3.cloned.1.call-done, f32[2048,256]{1,0:T(8,128)S(1)} %copy-done, f32[256]{0:T(256)S(1)} %multiply_reduce_fusion.1, f32[2048]{0:T(1024)S(1)} %multiply_reduce_fusion), kind=kOutput, calls=%fused_computation.6 | convolution fusion | flops 1612709888 | bytes 4465664 | tf_op jit(solution)/shard_map/dot_general | solution.py:14
  54.6 58.2 %all-gather.3.cloned.1.call-done = f32[2048,1024]{0,1:T(8,128)} async-done(((f32[2048,256]{0,1:T(8,128)}), f32[2048,1024]{0,1:T(8,128)}) %all-gather.3.cloned.1.call-update) | async-done | bytes 8388624 | tf_op jit(solution)/shard_map/all_gather | solution.py:45
  112.8 10.6 %fusion.38 = f32[1024,256]{1,0:T(8,128)} fusion(f32[2048,1024]{0,1:T(8,128)} %all-gather.3.cloned.1.call-done, f32[2048,256]{0,1:T(8,128)} %fusion.4), kind=kOutput, calls=%fused_computation.90 | convolution fusion | flops 6442450944 | bytes 11534336 | tf_op jit(solution)/shard_map/dot_general | solution.py:26
  123.5 27.4 %reduce-scatter.2.cloned.1.call-done = f32[256,256]{1,0:T(8,128)} async-done(((f32[1024,256]{1,0:T(8,128)}), f32[256,256]{1,0:T(8,128)}) %reduce-scatter.2.cloned.1.call-update) | async-done | bytes 262160 | tf_op jit(solution)/shard_map/reduce_scatter | solution.py:46
  150.9 50.9 %all-gather.5.cloned.1.call-done = f32[4096,256]{1,0:T(8,128)} async-done(((f32[256,256]{1,0:T(8,128)}), f32[4096,256]{1,0:T(8,128)}) %all-gather.5.cloned.1.call-update) | async-done | bytes 4194320 | tf_op jit(solution)/shard_map/all_gather | solution.py:48
  201.9 5.2 %copy.4 = f32[4,4,256,256]{2,0,3,1:T(4,128)} copy(f32[4,4,256,256]{3,2,1,0:T(8,128)} %bitcast.67) | data formatting | bytes 8388608 | tf_op jit(solution)/shard_map/reshape | solution.py:49
  207.1 5.1 %copy.7 = f32[128,8,4,256]{3,1,2,0:T(8,128)} copy(f32[128,8,4,256]{3,2,1,0:T(4,128)} %bitcast.66) | data formatting | bytes 8388608
  212.2 5.5 %copy.5 = f32[1024,1024]{1,0:T(8,128)} copy(f32[1024,1024]{0,1:T(8,128)} %bitcast.64) | data formatting | bytes 8388608 | tf_op jit(solution)/shard_map/reshape | solution.py:50
  224.1 11.7 %cholesky.223 = f32[128,128]{1,0:T(8,128)S(1)} custom-call(f32[128,128]{1,0:T(8,128)S(1)} %cholesky.580), custom_call_target="Cholesky" | custom-call | tf_op jit(solution)/shard_map/jit(cholesky)/cholesky | solution.py:51
  235.9 9.8 %custom-call.59 = f32[1,128,128]{1,2,0:T(8,128)S(1)} custom-call(f32[1,128,128]{2,1,0:T(8,128)S(1)} %get-tuple-element.26), custom_call_target="InvertDiagBlocksLowerTriangular" | custom-call | tf_op jit(solution)/shard_map/jit(cholesky)/cholesky | solution.py:51
  252.1 12.1 %cholesky.244 = f32[128,128]{1,0:T(8,128)S(1)} custom-call(f32[128,128]{1,0:T(8,128)S(1)} %cholesky.584), custom_call_target="Cholesky" | custom-call | tf_op jit(solution)/shard_map/jit(cholesky)/cholesky | solution.py:51
  264.9 9.8 %custom-call.60 = f32[1,128,128]{1,2,0:T(8,128)S(1)} custom-call(f32[1,128,128]{2,1,0:T(8,128)S(1)} %get-tuple-element.23), custom_call_target="InvertDiagBlocksLowerTriangular" | custom-call | tf_op jit(solution)/shard_map/jit(cholesky)/cholesky | solution.py:51
  278.0 11.7 %cholesky.468 = f32[128,128]{1,0:T(8,128)S(1)} custom-call(f32[128,128]{1,0:T(8,128)S(1)} %cholesky.589), custom_call_target="Cholesky" | custom-call | tf_op jit(solution)/shard_map/jit(cholesky)/cholesky | solution.py:51
  291.0 9.8 %custom-call.61 = f32[1,128,128]{1,2,0:T(8,128)S(1)} custom-call(f32[1,128,128]{2,1,0:T(8,128)S(1)} %get-tuple-element.20), custom_call_target="InvertDiagBlocksLowerTriangular" | custom-call | tf_op jit(solution)/shard_map/jit(cholesky)/cholesky | solution.py:51
  304.3 11.8 %cholesky.487 = f32[128,128]{1,0:T(8,128)S(1)} custom-call(f32[128,128]{1,0:T(8,128)S(1)} %cholesky.594), custom_call_target="Cholesky" | custom-call | tf_op jit(solution)/shard_map/jit(cholesky)/cholesky | solution.py:51
  317.5 9.8 %custom-call.62 = f32[1,128,128]{1,2,0:T(8,128)S(1)} custom-call(f32[1,128,128]{2,1,0:T(8,128)S(1)} %get-tuple-element.17), custom_call_target="InvertDiagBlocksLowerTriangular" | custom-call | tf_op jit(solution)/shard_map/jit(cholesky)/cholesky | solution.py:51
  330.7 11.7 %cholesky.506 = f32[128,128]{1,0:T(8,128)S(1)} custom-call(f32[128,128]{1,0:T(8,128)S(1)} %cholesky.599), custom_call_target="Cholesky" | custom-call | tf_op jit(solution)/shard_map/jit(cholesky)/cholesky | solution.py:51
  343.7 10.0 %custom-call.63 = f32[1,128,128]{1,2,0:T(8,128)S(1)} custom-call(f32[1,128,128]{2,1,0:T(8,128)S(1)} %get-tuple-element.14), custom_call_target="InvertDiagBlocksLowerTriangular" | custom-call | tf_op jit(solution)/shard_map/jit(cholesky)/cholesky | solution.py:51
  357.0 11.7 %cholesky.526 = f32[128,128]{1,0:T(8,128)S(1)} custom-call(f32[128,128]{1,0:T(8,128)S(1)} %cholesky.604), custom_call_target="Cholesky" | custom-call | tf_op jit(solution)/shard_map/jit(cholesky)/cholesky | solution.py:51
  370.0 9.8 %custom-call.64 = f32[1,128,128]{1,2,0:T(8,128)S(1)} custom-call(f32[1,128,128]{2,1,0:T(8,128)S(1)} %get-tuple-element.11), custom_call_target="InvertDiagBlocksLowerTriangular" | custom-call | tf_op jit(solution)/shard_map/jit(cholesky)/cholesky | solution.py:51
  382.8 11.9 %cholesky.546 = f32[128,128]{1,0:T(8,128)S(1)} custom-call(f32[128,128]{1,0:T(8,128)S(1)} %cholesky.609), custom_call_target="Cholesky" | custom-call | tf_op jit(solution)/shard_map/jit(cholesky)/cholesky | solution.py:51
  396.0 9.8 %custom-call.65 = f32[1,128,128]{1,2,0:T(8,128)S(1)} custom-call(f32[1,128,128]{2,1,0:T(8,128)S(1)} %get-tuple-element.8), custom_call_target="InvertDiagBlocksLowerTriangular" | custom-call | tf_op jit(solution)/shard_map/jit(cholesky)/cholesky | solution.py:51
  408.4 11.7 %cholesky.564 = f32[128,128]{1,0:T(8,128)S(1)} custom-call(f32[128,128]{1,0:T(8,128)S(1)} %convolution_subtract_fusion.6), custom_call_target="Cholesky" | custom-call | tf_op jit(solution)/shard_map/jit(cholesky)/cholesky | solution.py:51
  (55 shorter events, 50.7 us)
Async XLA Ops:
  6.5 43.4 %copy-start = (f32[2048,256]{1,0:T(8,128)S(1)}, f32[2048,256]{1,0:T(8,128)}, u32[]{:S(2)}) copy-start(f32[2048,256]{1,0:T(8,128)} %param.3) | copy-start | bytes 6291460
  6.5 42.3 %all-reduce.3.cloned.1.call-start = ((), (), s32[]{:S(2)}) async-start(), calls=%async_computation.1 | async-start | bytes 524288 | tf_op jit(solution)/shard_map/psum | solution.py:42
  10.4 102.5 %all-gather.3.cloned.1.call-start = ((), (), s32[]{:S(2)}) async-start(), calls=%async_computation.2 | async-start | bytes 10485760 | tf_op jit(solution)/shard_map/all_gather | solution.py:45
  54.6 96.4 %reduce-scatter.2.cloned.1.call-start = ((), (), s32[]{:S(2)}) async-start(), calls=%async_computation.3 | async-start | bytes 1310720 | tf_op jit(solution)/shard_map/reduce_scatter | solution.py:46
  123.5 78.4 %all-gather.5.cloned.1.call-start = ((), (), s32[]{:S(2)}) async-start(), calls=%async_computation.4 | async-start | bytes 4456448 | tf_op jit(solution)/shard_map/all_gather | solution.py:48
  222.2 1.9 copy-start.1
Sparse Core Ops, SparseCore 0:
  10.5 38.3 all-reduce.2
  54.7 58.1 all-gather.2
  123.6 27.2 reduce-scatter.1
  152.9 48.8 all-gather.4
where the time goes:
time: 444 us; the launch traced here: 437 us
  other arithmetic  181 us (41%)
  waiting for transfers between devices  173 us (39%)
  matrix products  42.1 us (9%)
  local copies, waits for them, and re-layouts  21.7 us (5%)
  between operations  18.6 us (4%)
    another operation x30, other arithmetic, local(): lower_factor = jnp.linalg.cholesky(gram)  172 us
    all_gather x1, waiting for transfers between devices, local(): lax.all_gather(own_panel, 'col', axis=1, tiled=True)  58.2 us
    all_gather x1, waiting for transfers between devices, local(): gathered = lax.all_gather(gram_part, ('dp', 'col'), axis=0, tiled=True)  50.9 us
    psum x1, waiting for transfers between devices, local(): centers = lax.psum(picked_rows, 'dp')  36.5 us
    reduce_scatter x1, waiting for transfers between devices, local(): gram_part = lax.psum_scatter(product, 'dp', scatter_dimension=0, tiled=True)  27.4 us
    another operation x14, matrix products, local(): lower_factor = jnp.linalg.cholesky(gram)  23.1 us
    dot_general x1, matrix products, cross_rows(): lax.dot_general(left_panel, right_panel, (((0,), (0,)), ((), ())), precis...  10.6 us
  transfers between devices with their start and end apart: 4, of which 4 were waited for; matrix products, arithmetic and copies ran while one was open for 0% of the time, Pallas kernels for 0%

commit v1 on v0

v1 whole, which is shorter than its diff:
```python
import functools

import jax
import jax.numpy as jnp
from jax import lax
from jax.experimental import pallas as pl
from jax.experimental.pallas import tpu as pltpu
from jax.sharding import PartitionSpec as P

LAND = 1024
NB = 128
PAIR = 2 * NB
STRIPS = NB // 8
BLOCKS = LAND // NB

F32 = jnp.float32
BF16 = jnp.bfloat16
precise = lax.Precision.HIGHEST


def nt(a, b):
    return lax.dot_general(a, b, (((1,), (1,)), ((), ())), precision=precise, preferred_element_type=F32)


def nt16(a, b):
    return lax.dot_general(a, b, (((1,), (1,)), ((), ())), preferred_element_type=F32)


def split3(x):
    high = x.astype(BF16)
    rest = x - high.astype(F32)
    mid = rest.astype(BF16)
    low = (rest - mid.astype(F32)).astype(BF16)
    return high, mid, low


def log2(n):
    bits = n.bit_length() - 1
    assert n == 1 << bits
    return bits


def mirror(k):
    return (2 << k) - 1


def gray(i):
    return i ^ (i >> 1)


def ungray(g, bits):
    i = g
    for s in range(1, bits):
        i = i ^ (g >> s)
    return i


def swap(x, axis, mask):
    n = lax.axis_size(axis)
    return lax.ppermute(x, axis, [(i, i ^ mask) for i in range(n)])


def column_groups(nx):
    if nx == 4:
        return [[(0,), (7,)], [(1,), (6,)], [(2,), (5,)], [(3,), (4,)]]
    assert nx == 2
    return [[(0, 1), (6, 7)], [(2, 3), (4, 5)]]


def group_blocks(group):
    return [(j, c) for cols in group for c in cols for j in range(c, BLOCKS)]


class Plan:
    def __init__(self, dp, col):
        self.dp, self.col = dp, col
        self.nx = col // 2
        self.xbits, self.zbits = log2(self.nx), log2(dp)
        self.groups = column_groups(self.nx)
        self.rows = len(group_blocks(self.groups[0])) * NB
        rows = self.rows // 2
        self.halved = 0
        while self.halved < self.zbits and rows % 16 == 0:
            rows //= 2
            self.halved += 1
        self.piece = rows
        self.pieces = 2 << self.halved

    def own_piece(self, col_index, dp_index):
        g = gray(dp_index)
        s = col_index & 1
        for k in range(self.halved):
            s = (s << 1) | ((g >> k) & 1)
        return s


def pick_kernel(lid_ref, pid_ref, points_ref, out_ref):
    matches = jnp.where(lid_ref[...] == pid_ref[...], 1.0, 0.0).astype(BF16)
    high, mid, low = split3(points_ref[...])
    dot = functools.partial(jnp.dot, preferred_element_type=F32)
    out_ref[...] = (dot(matches, high) + dot(matches, mid)) + dot(matches, low)


def pick(landmark_ids, point_ids, points):
    n = landmark_ids.shape[0]
    return pl.pallas_call(
        pick_kernel,
        out_shape=jax.ShapeDtypeStruct((n, points.shape[1]), F32),
        name="pick",
    )(landmark_ids.reshape(n, 1), point_ids.reshape(1, -1), points)


def gram_kernel(plan, where_ref, points_ref, centers_ref, out_ref, centers, panel, tall):
    col, me = where_ref[0], where_ref[1]
    land_cols = LAND // plan.col
    half, dim = points_ref.shape
    for r in range(plan.col):
        rx, rc = r & (plan.nx - 1), r >> plan.xbits
        x = ungray(gray(col >> 1) ^ rx, plan.xbits)
        owner = (x << 1) | ((col & 1) ^ rc)
        at = pl.multiple_of(owner * land_cols, land_cols)
        centers[pl.ds(at, land_cols), :] = centers_ref[r * land_cols : (r + 1) * land_cols, :]
    pts = points_ref[...]
    point_norms = nt(jnp.ones((8, dim), F32), pts * pts)[0:1, :]
    for b in range(LAND // PAIR):
        c = centers[b * PAIR : (b + 1) * PAIR, :]
        center_norms = jnp.sum(c * c, axis=1, keepdims=True)
        distance = point_norms + center_norms - 2.0 * nt(c, pts)
        panel[b * PAIR : (b + 1) * PAIR, :] = jnp.exp(distance * (-2.0 / dim))
    for x, group in enumerate(plan.groups):

        @pl.when((col >> 1) == x)
        def _():
            at = 0
            for cols in group:
                lo = cols[0] * NB
                product = nt(panel[lo:, :], panel[lo : lo + len(cols) * NB, :])
                for k, c in enumerate(cols):
                    rows = LAND - c * NB
                    tall[at : at + rows, :] = product[k * NB :, k * NB : (k + 1) * NB]
                    at += rows

    for r in range(plan.pieces):
        start = pl.multiple_of((me ^ r) * plan.piece, 8)
        out_ref[r * plan.piece : (r + 1) * plan.piece, :] = tall[pl.ds(start, plan.piece), :]


def gram_pieces(plan, where, points, centers):
    half = points.shape[0] // 2
    dim = points.shape[1]
    return pl.pallas_call(
        functools.partial(gram_kernel, plan),
        grid_spec=pltpu.PrefetchScalarGridSpec(
            num_scalar_prefetch=1,
            grid=(1,),
            in_specs=[
                pl.BlockSpec((half, dim), lambda i, where: (where[0] & 1, 0)),
                pl.BlockSpec((LAND, dim), lambda i, where: (0, 0)),
            ],
            out_specs=pl.BlockSpec((plan.rows, NB), lambda i, where: (0, 0)),
            scratch_shapes=[
                pltpu.VMEM((LAND, dim), F32),
                pltpu.VMEM((LAND, half), F32),
                pltpu.VMEM((plan.rows, NB), F32),
            ],
        ),
        out_shape=jax.ShapeDtypeStruct((plan.rows, NB), F32),
        name="gram",
    )(where, points, centers)


def lanecast(x, lane):
    index = jnp.full((8, NB), lane, jnp.int32)
    return jnp.take_along_axis(x, index, axis=1, mode="promise_in_bounds")


def rowcast(x, row):
    return jnp.broadcast_to(x[row : row + 1, :], (8, NB))


def eliminate(rows, s, lane, sub):
    own, lo = rows[s], 8 * s
    columns = [lanecast(own, lo + j) for j in range(8)]
    p = {(i, j): rowcast(columns[j], i) for j in range(8) for i in range(j + 1)}
    inside = (lane >= lo) & (lane < lo + 8)
    t = [jnp.where(inside, jnp.where(lane == lo + j, 1.0, 0.0), rowcast(own, j)) for j in range(8)]
    inverse = []
    for j in range(8):
        inverse.append(1.0 / p[j, j])
        for i in range(j + 1, 8):
            m = p[j, i] * inverse[j]
            for l in range(i, 8):
                p[i, l] = p[i, l] - m * p[j, l]
            t[i] = t[i] - m * t[j]
    scaled = t[0] * lax.rsqrt(p[0, 0])
    for j in range(1, 8):
        scaled = jnp.where(sub == j, t[j] * lax.rsqrt(p[j, j]), scaled)
    if s + 1 < STRIPS:
        v = [t[j] * inverse[j] for j in range(8)]
        for j in range(7, -1, -1):
            for i in range(j):
                v[i] = v[i] - (p[i, j] * inverse[i]) * v[j]
        for q in range(s + 1, STRIPS):
            columns = [lanecast(rows[q], lo + j) for j in range(8)]
            rest = jnp.where(inside, 0.0, rows[q])
            for j in range(7, -1, -1):
                rest = rest - columns[j] * v[j]
            rows[q] = rest
    return scaled


def factor_inverse(block, inverse):
    lane = lax.broadcasted_iota(jnp.int32, (8, NB), 1)
    sub = lax.broadcasted_iota(jnp.int32, (8, NB), 0)
    rows = [block[8 * q : 8 * q + 8, :] for q in range(STRIPS)]
    for s in range(STRIPS):
        scaled = eliminate(rows, s, lane, sub)
        inverse[8 * s : 8 * s + 8, :] = jnp.where(lane < 8 * (s + 1), scaled, 0.0)


def cholesky_kernel(plan, where_ref, pieces_ref, out_ref, tall, a, block, inv1, inv2, l21):
    col, me = where_ref[0], where_ref[1]
    zmask = (1 << plan.halved) - 1
    for r in range(plan.pieces * plan.nx):
        rz = r & zmask
        rx = (r >> plan.halved) & (plan.nx - 1)
        rc = r >> (plan.halved + plan.xbits)
        x = ungray(gray(col >> 1) ^ rx, plan.xbits)
        piece = me ^ ((rc << plan.halved) | rz)
        start = pl.multiple_of(x * plan.rows + piece * plan.piece, 8)
        tall[pl.ds(start, plan.piece), :] = pieces_ref[r * plan.piece : (r + 1) * plan.piece, :]
    at = 0
    for group in plan.groups:
        for j, c in group_blocks(group):
            a[j * NB : (j + 1) * NB, c * NB : (c + 1) * NB] = tall[at : at + NB, :]
            at += NB

    row = lax.broadcasted_iota(jnp.int32, (NB, NB), 0)
    column = lax.broadcasted_iota(jnp.int32, (NB, NB), 1)

    def step(k, carry):
        base = pl.multiple_of((k // 2) * PAIR, PAIR)
        first = (k % 2) == 0
        for t in range(LAND // PAIR):
            lo = t * PAIR

            @pl.when(k == 2 * t)
            def _():
                if t:
                    update = nt(a[lo:, :lo], a[lo : lo + PAIR, :lo])
                    a[lo:, lo : lo + PAIR] = a[lo:, lo : lo + PAIR] - update
                block[...] = a[lo : lo + NB, lo : lo + NB]

        @pl.when(jnp.logical_not(first))
        def _():
            below = nt(a[pl.ds(base + NB, NB), pl.ds(base, NB)], inv2[...])
            l21[...] = below
            inv1[...] = inv2[...]
            block[...] = a[pl.ds(base + NB, NB), pl.ds(base + NB, NB)] - nt(below, below)

        factor_inverse(block, inv2)

        for t in range(LAND // PAIR):
            lo = t * PAIR

            @pl.when(k == 2 * t + 1)
            def _():
                left = nt(a[lo:, lo : lo + NB], inv1[...])
                right = a[lo + NB :, lo + NB : lo + PAIR] - nt(left[NB:, :], l21[...])
                right = nt(right, inv2[...])
                a[lo : lo + NB, lo : lo + NB] = jnp.where(column <= row, left[:NB, :], 0.0)
                a[lo + NB :, lo : lo + NB] = left[NB:, :]
                a[lo + NB : lo + PAIR, lo + NB : lo + PAIR] = jnp.where(column <= row, right[:NB, :], 0.0)
                if lo + PAIR < LAND:
                    a[lo + PAIR :, lo + NB : lo + PAIR] = right[NB:, :]

        return carry

    lax.fori_loop(0, BLOCKS, step, 0)

    width = LAND // plan.col
    out_ref[...] = jnp.zeros(out_ref.shape, F32)
    for c in range(plan.col):

        @pl.when(col == c)
        def _():
            for j in range(width // NB):
                at = c * width + j * NB
                for i in range(at // NB + 1):
                    out_ref[i * NB : (i + 1) * NB, j * NB : (j + 1) * NB] = a[at : at + NB, i * NB : (i + 1) * NB].T


def factor(plan, where, pieces):
    total = plan.rows * plan.nx
    width = LAND // plan.col
    return pl.pallas_call(
        functools.partial(cholesky_kernel, plan),
        grid_spec=pltpu.PrefetchScalarGridSpec(
            num_scalar_prefetch=1,
            grid=(1,),
            in_specs=[pl.BlockSpec((total, NB), lambda i, where: (0, 0))],
            out_specs=pl.BlockSpec((LAND, width), lambda i, where: (0, 0)),
            scratch_shapes=[
                pltpu.VMEM((total, NB), F32),
                pltpu.VMEM((LAND, LAND), F32),
                pltpu.VMEM((NB, NB), F32),
                pltpu.VMEM((NB, NB), F32),
                pltpu.VMEM((NB, NB), F32),
                pltpu.VMEM((NB, NB), F32),
            ],
        ),
        out_shape=jax.ShapeDtypeStruct((LAND, width), F32),
        name="factor",
    )(where, pieces)


def local(points, point_ids, landmark_ids):
    plan = Plan(lax.axis_size("dp"), lax.axis_size("col"))
    col_index, dp_index = lax.axis_index("col"), lax.axis_index("dp")
    where = jnp.stack([col_index, plan.own_piece(col_index, dp_index)]).astype(jnp.int32)

    centers = pick(landmark_ids, point_ids, points)
    for k in range(plan.zbits):
        centers = centers + swap(centers, "dp", mirror(k))
    for k in range(plan.xbits):
        centers = jnp.concatenate([centers, swap(centers, "col", 2 * mirror(k))])
    centers = jnp.concatenate([centers, swap(centers, "col", 1)])

    held = gram_pieces(plan, where, points, centers)
    half = plan.rows // 2
    held = held[:half] + swap(held[half:], "col", 1)
    for k in range(plan.halved):
        half = half // 2
        held = held[:half] + swap(held[half:], "dp", mirror(k))
    for k in range(plan.halved, plan.zbits):
        held = held + swap(held, "dp", mirror(k))
    for k in reversed(range(plan.halved)):
        held = jnp.concatenate([held, swap(held, "dp", mirror(k))])
    for k in range(plan.xbits):
        held = jnp.concatenate([held, swap(held, "col", 2 * mirror(k))])
    held = jnp.concatenate([held, swap(held, "col", 1)])
    return factor(plan, where, held)


def solution(mesh):
    in_specs = (P(("groups", "dp"), None), P(("groups", "dp")), P(("groups", "col")))
    out_specs = P("groups", "col")
    return jax.shard_map(local, mesh=mesh, in_specs=in_specs, out_specs=out_specs, check_vma=False)
```

time: 444 us -> 149 us (0.34); the launches traced: 437 us -> 149 us
  other arithmetic: 181 us -> 4.01 us
  waiting for transfers between devices: 173 us -> 60.6 us
  Pallas kernels: 0 us -> 57.1 us
  matrix products: 42.1 us -> 0 us
  starting transfers between devices: 0.13 us -> 22.5 us
  between operations: 18.6 us -> 0.12 us
  local copies, waits for them, and re-layouts: 21.7 us -> 4.17 us
    another operation x30 -> x1, other arithmetic: 172 us -> 0.6 us  [local(): jnp.stack([col_index, plan.own_piece(col_index, dp_index)])]
    all_gather x2 -> x0, waiting for transfers between devices: 109 us -> none  [the longest x1 58.2 us: local(): lax.all_gather(own_panel, 'col', axis=1, tiled=True)]
    ppermute x0 -> x11, waiting for transfers between devices: none -> 60.6 us  [swap(): return lax.ppermute(x, axis, [(i, i ^ mask) for i in range(n)])]
    pallas_call x0 -> x3, Pallas kernels: none -> 57.1 us  [the longest x1 41.2 us: factor(): pl.pallas_call(functools.partial(cholesky_kernel, plan), grid_spec=pltpu....]
    psum x1 -> x0, waiting for transfers between devices: 36.5 us -> none  [local(): centers = lax.psum(picked_rows, 'dp')]
    reduce_scatter x1 -> x0, waiting for transfers between devices: 27.4 us -> none  [local(): gram_part = lax.psum_scatter(product, 'dp', scatter_dimension=0, tiled=True)]
    another operation x14 -> x0, matrix products: 23.1 us -> none  [local(): lower_factor = jnp.linalg.cholesky(gram)]
    ppermute x0 -> x11, starting transfers between devices: none -> 22.5 us  [swap(): return lax.ppermute(x, axis, [(i, i ^ mask) for i in range(n)])]
  transfers between devices with their start and end apart: 4 -> 11, of which waited for: 4 -> 11; matrix products, arithmetic and copies ran while one was open for 0% -> 0% of each run, Pallas kernels for 0% -> 0%
where the time goes in v1:
time: 149 us
  waiting for transfers between devices  60.6 us (41%)
  Pallas kernels  57.1 us (38%)
  starting transfers between devices  22.5 us (15%)
  local copies, waits for them, and re-layouts  4.17 us (3%)
  other arithmetic  4.01 us (3%)
    ppermute x11, waiting for transfers between devices, swap(): return lax.ppermute(x, axis, [(i, i ^ mask) for i in range(n)])  60.6 us
    pallas_call x1, Pallas kernels, factor(): pl.pallas_call(functools.partial(cholesky_kernel, plan), grid_spec=pltpu....  41.2 us
    ppermute x11, starting transfers between devices, swap(): return lax.ppermute(x, axis, [(i, i ^ mask) for i in range(n)])  22.5 us
    pallas_call x1, Pallas kernels, gram_pieces(): pl.pallas_call(functools.partial(gram_kernel, plan), grid_spec=pltpu.Pref...  12.4 us
    pallas_call x1, Pallas kernels, pick(): pl.pallas_call(pick_kernel, out_shape=jax.ShapeDtypeStruct((n, points.sha...  3.47 us
  transfers between devices with their start and end apart: 11, of which 11 were waited for; matrix products, arithmetic and copies ran while one was open for 0% of the time, Pallas kernels for 0%

profile of v1, /device:TPU:0, one launch (start us, length us, event | category | flops | bytes accessed | tf_op | source)
XLA Modules:
  0.0 148.5 jit_solution(469076790815959037)
XLA Ops:
  0.0 1.5 copy.4.lid_ref
  1.5 3.5 %pick.1 = f32[256,256]{1,0:T(8,128)} custom-call(s32[256,1]{1,0:T(8,128)} %copy.4.lid_ref, s32[1,2048]{1,0:T(1,128)} %bitcast.4, f32[2048,256]{1,0:T(8,128)} %points_ref.3), custom_call_target="tpu_custom_call" | custom-call | tf_op jit(solution)/shard_map/pick/pallas_call | solution.py:106
  4.9 3.1 %collective-permute-start = (f32[256,256]{1,0:T(8,128)}, f32[256,256]{1,0:T(8,128)S(1)}, u32[]{:S(2)}, u32[]{:S(2)}) collective-permute-start(f32[256,256]{1,0:T(8,128)} %pick.1), channel_id=1, source_target_pairs={{0,4},{4,0},{8,12},{12,8},{1,5},{5,1},{9,13},{13,9},{2,6},{6,2},{1... | collective-permute-start | bytes 786440 | tf_op jit(solution)/shard_map/ppermute | solution.py:60
  8.0 6.5 %collective-permute-done = f32[256,256]{1,0:T(8,128)S(1)} collective-permute-done((f32[256,256]{1,0:T(8,128)}, f32[256,256]{1,0:T(8,128)S(1)}, u32[]{:S(2)}, u32[]{:S(2)}) %collective-permute-start) | collective-permute-done | bytes 262176 | tf_op jit(solution)/shard_map/ppermute | solution.py:60
  15.5 3.8 %collective-permute-start.1 = (f32[256,256]{1,0:T(8,128)S(1)}, f32[256,256]{1,0:T(8,128)S(1)}, u32[]{:S(2)}, u32[]{:S(2)}) collective-permute-start(f32[256,256]{1,0:T(8,128)S(1)} %add.15), channel_id=1, source_target_pairs={{0,12},{4,8},{8,4},{12,0},{1,13},{5,9},{9,5},{13,1},{2,14},{6,10},... | collective-permute-start | bytes 786440 | tf_op jit(solution)/shard_map/ppermute | solution.py:60
  19.3 5.6 %collective-permute-done.1 = f32[256,256]{1,0:T(8,128)S(1)} collective-permute-done((f32[256,256]{1,0:T(8,128)S(1)}, f32[256,256]{1,0:T(8,128)S(1)}, u32[]{:S(2)}, u32[]{:S(2)}) %collective-permute-start.1) | collective-permute-done | bytes 262176 | tf_op jit(solution)/shard_map/ppermute | solution.py:60
  25.0 1.5 %collective-permute-start.2 = (f32[256,256]{1,0:T(8,128)S(1)}, f32[256,256]{1,0:T(8,128)S(1)}, u32[]{:S(2)}, u32[]{:S(2)}) collective-permute-start(f32[256,256]{1,0:T(8,128)S(1)} %add.16), channel_id=1, source_target_pairs={{0,2},{1,3},{2,0},{3,1},{4,6},{5,7},{6,4},{7,5},{8,10},{9,11},{10,... | collective-permute-start | bytes 786440 | tf_op jit(solution)/shard_map/ppermute | solution.py:60
  26.5 5.2 %collective-permute-done.2 = f32[256,256]{1,0:T(8,128)S(1)} collective-permute-done((f32[256,256]{1,0:T(8,128)S(1)}, f32[256,256]{1,0:T(8,128)S(1)}, u32[]{:S(2)}, u32[]{:S(2)}) %collective-permute-start.2) | collective-permute-done | bytes 262176 | tf_op jit(solution)/shard_map/ppermute | solution.py:60
  32.4 1.3 collective-permute-done.3
  34.7 12.4 %gram.1 = f32[2304,128]{1,0:T(8,128)} custom-call(s32[2]{0:T(128)} %pad_add_fusion.where_ref, f32[2048,256]{1,0:T(8,128)} %points_ref.3, f32[1024,256]{1,0:T(8,128)} %pad_maximum_fusion.1.centers_ref), custom_call_target="tpu_custom_call" | custom-call | tf_op jit(solution)/shard_map/gram/pallas_call | solution.py:151
  48.4 1.9 %collective-permute-done.4 = f32[1152,128]{1,0:T(8,128)S(1)} collective-permute-done((f32[1152,128]{1,0:T(8,128)S(1)}, f32[1152,128]{1,0:T(8,128)S(1)}, u32[]{:S(2)}, u32[]{:S(2)}) %collective-permute-start.4) | collective-permute-done | bytes 589856 | tf_op jit(solution)/shard_map/ppermute | solution.py:60
  51.5 6.0 %collective-permute-start.5 = (f32[576,128]{1,0:T(8,128)S(1)}, f32[576,128]{1,0:T(8,128)S(1)}, u32[]{:S(2)}, u32[]{:S(2)}) collective-permute-start(f32[576,128]{1,0:T(8,128)S(1)} %slice.27), channel_id=1, source_target_pairs={{0,4},{4,0},{8,12},{12,8},{1,5},{5,1},{9,13},{13,9},{2,6},{6,2},{1... | collective-permute-start | bytes 884744 | tf_op jit(solution)/shard_map/ppermute | solution.py:60
  57.4 7.3 %collective-permute-done.5 = f32[576,128]{1,0:T(8,128)S(1)} collective-permute-done((f32[576,128]{1,0:T(8,128)S(1)}, f32[576,128]{1,0:T(8,128)S(1)}, u32[]{:S(2)}, u32[]{:S(2)}) %collective-permute-start.5) | collective-permute-done | bytes 294944 | tf_op jit(solution)/shard_map/ppermute | solution.py:60
  64.8 1.6 %collective-permute-start.6 = (f32[288,128]{1,0:T(8,128)S(1)}, f32[288,128]{1,0:T(8,128)S(1)}, u32[]{:S(2)}, u32[]{:S(2)}) collective-permute-start(f32[288,128]{1,0:T(8,128)S(1)} %slice.29), channel_id=1, source_target_pairs={{0,12},{4,8},{8,4},{12,0},{1,13},{5,9},{9,5},{13,1},{2,14},{6,10},... | collective-permute-start | bytes 442376 | tf_op jit(solution)/shard_map/ppermute | solution.py:60
  66.4 5.7 %collective-permute-done.6 = f32[288,128]{1,0:T(8,128)S(1)} collective-permute-done((f32[288,128]{1,0:T(8,128)S(1)}, f32[288,128]{1,0:T(8,128)S(1)}, u32[]{:S(2)}, u32[]{:S(2)}) %collective-permute-start.6) | collective-permute-done | bytes 147488 | tf_op jit(solution)/shard_map/ppermute | solution.py:60
  72.1 1.6 %collective-permute-start.7 = (f32[288,128]{1,0:T(8,128)S(1)}, f32[288,128]{1,0:T(8,128)S(1)}, u32[]{:S(2)}, u32[]{:S(2)}) collective-permute-start(f32[288,128]{1,0:T(8,128)S(1)} %get-tuple-element.6), channel_id=1, source_target_pairs={{0,12},{4,8},{8,4},{12,0},{1,13},{5,9},{9,5},{13,1},{2,14},{6,10},... | collective-permute-start | bytes 442376 | tf_op jit(solution)/shard_map/ppermute | solution.py:60
  73.7 5.5 %collective-permute-done.7 = f32[288,128]{1,0:T(8,128)S(1)} collective-permute-done((f32[288,128]{1,0:T(8,128)S(1)}, f32[288,128]{1,0:T(8,128)S(1)}, u32[]{:S(2)}, u32[]{:S(2)}) %collective-permute-start.7) | collective-permute-done | bytes 147488 | tf_op jit(solution)/shard_map/ppermute | solution.py:60
  79.3 3.0 %collective-permute-start.8 = (f32[576,128]{1,0:T(8,128)S(1)}, f32[576,128]{1,0:T(8,128)S(1)}, u32[]{:S(2)}, u32[]{:S(2)}) collective-permute-start(f32[576,128]{1,0:T(8,128)S(1)} %pad_maximum_fusion.4), channel_id=1, source_target_pairs={{0,4},{4,0},{8,12},{12,8},{1,5},{5,1},{9,13},{13,9},{2,6},{6,2},{1... | collective-permute-start | bytes 884744 | tf_op jit(solution)/shard_map/ppermute | solution.py:60
  82.2 6.5 %collective-permute-done.8 = f32[576,128]{1,0:T(8,128)S(1)} collective-permute-done((f32[576,128]{1,0:T(8,128)S(1)}, f32[576,128]{1,0:T(8,128)S(1)}, u32[]{:S(2)}, u32[]{:S(2)}) %collective-permute-start.8) | collective-permute-done | bytes 294944 | tf_op jit(solution)/shard_map/ppermute | solution.py:60
  88.8 1.6 %collective-permute-start.9 = (f32[1152,128]{1,0:T(8,128)S(1)}, f32[1152,128]{1,0:T(8,128)S(1)}, u32[]{:S(2)}, u32[]{:S(2)}) collective-permute-start(f32[1152,128]{1,0:T(8,128)S(1)} %pad_maximum_fusion.2), channel_id=1, source_target_pairs={{0,2},{1,3},{2,0},{3,1},{4,6},{5,7},{6,4},{7,5},{8,10},{9,11},{10,... | collective-permute-start | bytes 1769480 | tf_op jit(solution)/shard_map/ppermute | solution.py:60
  90.4 12.5 %collective-permute-done.9 = f32[1152,128]{1,0:T(8,128)S(1)} collective-permute-done((f32[1152,128]{1,0:T(8,128)S(1)}, f32[1152,128]{1,0:T(8,128)S(1)}, u32[]{:S(2)}, u32[]{:S(2)}) %collective-permute-start.9) | collective-permute-done | bytes 589856 | tf_op jit(solution)/shard_map/ppermute | solution.py:60
  103.1 2.7 %collective-permute-done.10 = f32[2304,128]{1,0:T(8,128)S(1)} collective-permute-done((f32[2304,128]{1,0:T(8,128)S(1)}, f32[2304,128]{1,0:T(8,128)S(1)}, u32[]{:S(2)}, u32[]{:S(2)}) %collective-permute-start.10) | collective-permute-done | bytes 1179680 | tf_op jit(solution)/shard_map/ppermute | solution.py:60
  105.9 1.4 copy-done
  107.3 41.2 %factor.1 = f32[1024,256]{1,0:T(8,128)} custom-call(s32[2]{0:T(128)} %pad_add_fusion.where_ref, f32[4608,128]{1,0:T(8,128)} %copy-done), custom_call_target="tpu_custom_call" | custom-call | tf_op jit(solution)/shard_map/factor/pallas_call | solution.py:296
  (22 shorter events, 5.6 us)
Async XLA Ops:
  4.9 9.6 %collective-permute-start = (f32[256,256]{1,0:T(8,128)}, f32[256,256]{1,0:T(8,128)S(1)}, u32[]{:S(2)}, u32[]{:S(2)}) collective-permute-start(f32[256,256]{1,0:T(8,128)} %pick.1), channel_id=1, source_target_pairs={{0,4},{4,0},{8,12},{12,8},{1,5},{5,1},{9,13},{13,9},{2,6},{6,2},{1... | collective-permute-start | bytes 786440 | tf_op jit(solution)/shard_map/ppermute | solution.py:60
  15.5 9.4 %collective-permute-start.1 = (f32[256,256]{1,0:T(8,128)S(1)}, f32[256,256]{1,0:T(8,128)S(1)}, u32[]{:S(2)}, u32[]{:S(2)}) collective-permute-start(f32[256,256]{1,0:T(8,128)S(1)} %add.15), channel_id=1, source_target_pairs={{0,12},{4,8},{8,4},{12,0},{1,13},{5,9},{9,5},{13,1},{2,14},{6,10},... | collective-permute-start | bytes 786440 | tf_op jit(solution)/shard_map/ppermute | solution.py:60
  25.0 6.7 %collective-permute-start.2 = (f32[256,256]{1,0:T(8,128)S(1)}, f32[256,256]{1,0:T(8,128)S(1)}, u32[]{:S(2)}, u32[]{:S(2)}) collective-permute-start(f32[256,256]{1,0:T(8,128)S(1)} %add.16), channel_id=1, source_target_pairs={{0,2},{1,3},{2,0},{3,1},{4,6},{5,7},{6,4},{7,5},{8,10},{9,11},{10,... | collective-permute-start | bytes 786440 | tf_op jit(solution)/shard_map/ppermute | solution.py:60
  31.7 2.0 %collective-permute-start.3 = (f32[512,256]{1,0:T(8,128)S(1)}, f32[512,256]{1,0:T(8,128)S(1)}, u32[]{:S(2)}, u32[]{:S(2)}) collective-permute-start(f32[512,256]{1,0:T(8,128)S(1)} %pad_maximum_fusion.3), channel_id=1, source_target_pairs={{0,1},{1,0},{2,3},{3,2},{4,5},{5,4},{6,7},{7,6},{8,9},{9,8},{10,11... | collective-permute-start | bytes 1572872 | tf_op jit(solution)/shard_map/ppermute | solution.py:60
  48.2 2.1 %collective-permute-start.4 = (f32[1152,128]{1,0:T(8,128)S(1)}, f32[1152,128]{1,0:T(8,128)S(1)}, u32[]{:S(2)}, u32[]{:S(2)}) collective-permute-start(f32[1152,128]{1,0:T(8,128)S(1)} %slice.25), channel_id=1, source_target_pairs={{0,1},{1,0},{2,3},{3,2},{4,5},{5,4},{6,7},{7,6},{8,9},{9,8},{10,11... | collective-permute-start | bytes 1769480 | tf_op jit(solution)/shard_map/ppermute | solution.py:60
  51.5 13.3 %collective-permute-start.5 = (f32[576,128]{1,0:T(8,128)S(1)}, f32[576,128]{1,0:T(8,128)S(1)}, u32[]{:S(2)}, u32[]{:S(2)}) collective-permute-start(f32[576,128]{1,0:T(8,128)S(1)} %slice.27), channel_id=1, source_target_pairs={{0,4},{4,0},{8,12},{12,8},{1,5},{5,1},{9,13},{13,9},{2,6},{6,2},{1... | collective-permute-start | bytes 884744 | tf_op jit(solution)/shard_map/ppermute | solution.py:60
  64.8 7.3 %collective-permute-start.6 = (f32[288,128]{1,0:T(8,128)S(1)}, f32[288,128]{1,0:T(8,128)S(1)}, u32[]{:S(2)}, u32[]{:S(2)}) collective-permute-start(f32[288,128]{1,0:T(8,128)S(1)} %slice.29), channel_id=1, source_target_pairs={{0,12},{4,8},{8,4},{12,0},{1,13},{5,9},{9,5},{13,1},{2,14},{6,10},... | collective-permute-start | bytes 442376 | tf_op jit(solution)/shard_map/ppermute | solution.py:60
  72.1 7.1 %collective-permute-start.7 = (f32[288,128]{1,0:T(8,128)S(1)}, f32[288,128]{1,0:T(8,128)S(1)}, u32[]{:S(2)}, u32[]{:S(2)}) collective-permute-start(f32[288,128]{1,0:T(8,128)S(1)} %get-tuple-element.6), channel_id=1, source_target_pairs={{0,12},{4,8},{8,4},{12,0},{1,13},{5,9},{9,5},{13,1},{2,14},{6,10},... | collective-permute-start | bytes 442376 | tf_op jit(solution)/shard_map/ppermute | solution.py:60
  79.3 9.5 %collective-permute-start.8 = (f32[576,128]{1,0:T(8,128)S(1)}, f32[576,128]{1,0:T(8,128)S(1)}, u32[]{:S(2)}, u32[]{:S(2)}) collective-permute-start(f32[576,128]{1,0:T(8,128)S(1)} %pad_maximum_fusion.4), channel_id=1, source_target_pairs={{0,4},{4,0},{8,12},{12,8},{1,5},{5,1},{9,13},{13,9},{2,6},{6,2},{1... | collective-permute-start | bytes 884744 | tf_op jit(solution)/shard_map/ppermute | solution.py:60
  88.8 14.0 %collective-permute-start.9 = (f32[1152,128]{1,0:T(8,128)S(1)}, f32[1152,128]{1,0:T(8,128)S(1)}, u32[]{:S(2)}, u32[]{:S(2)}) collective-permute-start(f32[1152,128]{1,0:T(8,128)S(1)} %pad_maximum_fusion.2), channel_id=1, source_target_pairs={{0,2},{1,3},{2,0},{3,1},{4,6},{5,7},{6,4},{7,5},{8,10},{9,11},{10,... | collective-permute-start | bytes 1769480 | tf_op jit(solution)/shard_map/ppermute | solution.py:60
  102.9 2.9 %collective-permute-start.10 = (f32[2304,128]{1,0:T(8,128)S(1)}, f32[2304,128]{1,0:T(8,128)S(1)}, u32[]{:S(2)}, u32[]{:S(2)}) collective-permute-start(f32[2304,128]{1,0:T(8,128)S(1)} %pad_maximum_fusion), channel_id=1, source_target_pairs={{0,1},{1,0},{2,3},{3,2},{4,5},{5,4},{6,7},{7,6},{8,9},{9,8},{10,11... | collective-permute-start | bytes 3538952 | tf_op jit(solution)/shard_map/ppermute | solution.py:60
  105.9 1.4 copy-start

commit v2 on v1

--- a/solution.py
+++ b/solution.py
@@ -24,6 +24,11 @@
 
 def nt16(a, b):
     return lax.dot_general(a, b, (((1,), (1,)), ((), ())), preferred_element_type=F32)
+
+
+def split2(x):
+    high = x.astype(BF16)
+    return high, (x - high.astype(F32)).astype(BF16)
 
 
 def split3(x):
@@ -106,11 +111,13 @@
     return pl.pallas_call(
         pick_kernel,
         out_shape=jax.ShapeDtypeStruct((n, points.shape[1]), F32),
+        out_specs=pl.BlockSpec(memory_space=pltpu.VMEM),
+        compiler_params=pltpu.CompilerParams(vmem_limit_bytes=36 << 20),
         name="pick",
     )(landmark_ids.reshape(n, 1), point_ids.reshape(1, -1), points)
 
 
-def gram_kernel(plan, where_ref, points_ref, centers_ref, out_ref, centers, panel, tall):
+def gram_kernel(plan, where_ref, points_ref, centers_ref, kept_ref, sent_ref, centers, panel_high, panel_mid, tall):
     col, me = where_ref[0], where_ref[1]
     land_cols = LAND // plan.col
     half, dim = points_ref.shape
@@ -122,11 +129,17 @@
         centers[pl.ds(at, land_cols), :] = centers_ref[r * land_cols : (r + 1) * land_cols, :]
     pts = points_ref[...]
     point_norms = nt(jnp.ones((8, dim), F32), pts * pts)[0:1, :]
+    high, mid, low = split3(pts)
+    right = jnp.concatenate([low, mid, high, mid, high, high], axis=1)
     for b in range(LAND // PAIR):
-        c = centers[b * PAIR : (b + 1) * PAIR, :]
+        block = slice(b * PAIR, (b + 1) * PAIR)
+        c = centers[block, :]
         center_norms = jnp.sum(c * c, axis=1, keepdims=True)
-        distance = point_norms + center_norms - 2.0 * nt(c, pts)
-        panel[b * PAIR : (b + 1) * PAIR, :] = jnp.exp(distance * (-2.0 / dim))
+        high, mid, low = split3(c)
+        inner = nt16(jnp.concatenate([high, mid, low, high, mid, high], axis=1), right)
+        distance = point_norms + center_norms - 2.0 * inner
+        values = jnp.exp(distance * (-2.0 / dim))
+        panel_high[block, :], panel_mid[block, :] = split2(values)
     for x, group in enumerate(plan.groups):
 
         @pl.when((col >> 1) == x)
@@ -134,7 +147,11 @@
             at = 0
             for cols in group:
                 lo = cols[0] * NB
-                product = nt(panel[lo:, :], panel[lo : lo + len(cols) * NB, :])
+                some = slice(lo, lo + len(cols) * NB)
+                product = nt16(
+                    jnp.concatenate([panel_high[lo:, :], panel_mid[lo:, :], panel_high[lo:, :]], axis=1),
+                    jnp.concatenate([panel_mid[some, :], panel_high[some, :], panel_high[some, :]], axis=1),
+                )
                 for k, c in enumerate(cols):
                     rows = LAND - c * NB
                     tall[at : at + rows, :] = product[k * NB :, k * NB : (k + 1) * NB]
@@ -142,7 +159,8 @@
 
     for r in range(plan.pieces):
         start = pl.multiple_of((me ^ r) * plan.piece, 8)
-        out_ref[r * plan.piece : (r + 1) * plan.piece, :] = tall[pl.ds(start, plan.piece), :]
+        out, q = (kept_ref, r) if r < plan.pieces // 2 else (sent_ref, r - plan.pieces // 2)
+        out[q * plan.piece : (q + 1) * plan.piece, :] = tall[pl.ds(start, plan.piece), :]
 
 
 def gram_pieces(plan, where, points, centers):
@@ -155,16 +173,18 @@
             grid=(1,),
             in_specs=[
                 pl.BlockSpec((half, dim), lambda i, where: (where[0] & 1, 0)),
-                pl.BlockSpec((LAND, dim), lambda i, where: (0, 0)),
+                pl.BlockSpec(memory_space=pltpu.VMEM),
             ],
-            out_specs=pl.BlockSpec((plan.rows, NB), lambda i, where: (0, 0)),
+            out_specs=[pl.BlockSpec(memory_space=pltpu.VMEM)] * 2,
             scratch_shapes=[
                 pltpu.VMEM((LAND, dim), F32),
-                pltpu.VMEM((LAND, half), F32),
+                pltpu.VMEM((LAND, half), BF16),
+                pltpu.VMEM((LAND, half), BF16),
                 pltpu.VMEM((plan.rows, NB), F32),
             ],
         ),
-        out_shape=jax.ShapeDtypeStruct((plan.rows, NB), F32),
+        out_shape=[jax.ShapeDtypeStruct((plan.rows // 2, NB), F32)] * 2,
+        compiler_params=pltpu.CompilerParams(vmem_limit_bytes=36 << 20),
         name="gram",
     )(where, points, centers)
 
@@ -218,17 +238,15 @@
         inverse[8 * s : 8 * s + 8, :] = jnp.where(lane < 8 * (s + 1), scaled, 0.0)
 
 
-def cholesky_kernel(plan, where_ref, pieces_ref, out_ref, tall, a, block, inv1, inv2, l21):
+def cholesky_kernel(plan, where_ref, here0, here1, there0, there1, out_ref, tall, a, block, inv1, inv2, l21):
     col, me = where_ref[0], where_ref[1]
-    zmask = (1 << plan.halved) - 1
-    for r in range(plan.pieces * plan.nx):
-        rz = r & zmask
-        rx = (r >> plan.halved) & (plan.nx - 1)
-        rc = r >> (plan.halved + plan.xbits)
-        x = ungray(gray(col >> 1) ^ rx, plan.xbits)
-        piece = me ^ ((rc << plan.halved) | rz)
-        start = pl.multiple_of(x * plan.rows + piece * plan.piece, 8)
-        tall[pl.ds(start, plan.piece), :] = pieces_ref[r * plan.piece : (r + 1) * plan.piece, :]
+    low = plan.halved - 1
+    for rc, rz, pieces_ref in ((0, 0, here0), (0, 1, here1), (1, 0, there0), (1, 1, there1)):
+        for r in range(plan.nx << low):
+            x = ungray(gray(col >> 1) ^ (r >> low), plan.xbits)
+            piece = me ^ ((rc << plan.halved) | (rz << low) | (r & ((1 << low) - 1)))
+            start = pl.multiple_of(x * plan.rows + piece * plan.piece, 8)
+            tall[pl.ds(start, plan.piece), :] = pieces_ref[r * plan.piece : (r + 1) * plan.piece, :]
     at = 0
     for group in plan.groups:
         for j, c in group_blocks(group):
@@ -290,7 +308,7 @@
                     out_ref[i * NB : (i + 1) * NB, j * NB : (j + 1) * NB] = a[at : at + NB, i * NB : (i + 1) * NB].T
 
 
-def factor(plan, where, pieces):
+def factor(plan, where, parts):
     total = plan.rows * plan.nx
     width = LAND // plan.col
     return pl.pallas_call(
@@ -298,7 +316,7 @@
         grid_spec=pltpu.PrefetchScalarGridSpec(
             num_scalar_prefetch=1,
             grid=(1,),
-            in_specs=[pl.BlockSpec((total, NB), lambda i, where: (0, 0))],
+            in_specs=[pl.BlockSpec(memory_space=pltpu.VMEM)] * 4,
             out_specs=pl.BlockSpec((LAND, width), lambda i, where: (0, 0)),
             scratch_shapes=[
                 pltpu.VMEM((total, NB), F32),
@@ -310,8 +328,9 @@
             ],
         ),
         out_shape=jax.ShapeDtypeStruct((LAND, width), F32),
+        compiler_params=pltpu.CompilerParams(vmem_limit_bytes=28 << 20),
         name="factor",
-    )(where, pieces)
+    )(where, *parts)
 
 
 def local(points, point_ids, landmark_ids):
@@ -320,26 +339,33 @@
     where = jnp.stack([col_index, plan.own_piece(col_index, dp_index)]).astype(jnp.int32)
 
     centers = pick(landmark_ids, point_ids, points)
-    for k in range(plan.zbits):
-        centers = centers + swap(centers, "dp", mirror(k))
-    for k in range(plan.xbits):
-        centers = jnp.concatenate([centers, swap(centers, "col", 2 * mirror(k))])
+    first, second = jnp.split(centers, 2)
+    steps = list(range(plan.zbits))
+    for k, other in zip(steps, [1, 0] + steps[2:]):
+        first = first + swap(first, "dp", mirror(k))
+        second = second + swap(second, "dp", mirror(other))
+    centers = over_x(plan, jnp.concatenate([first, second]))
     centers = jnp.concatenate([centers, swap(centers, "col", 1)])
 
-    held = gram_pieces(plan, where, points, centers)
-    half = plan.rows // 2
-    held = held[:half] + swap(held[half:], "col", 1)
+    kept, sent = gram_pieces(plan, where, points, centers)
+    held = kept + swap(sent, "col", 1)
     for k in range(plan.halved):
-        half = half // 2
+        half = held.shape[0] // 2
         held = held[:half] + swap(held[half:], "dp", mirror(k))
     for k in range(plan.halved, plan.zbits):
         held = held + swap(held, "dp", mirror(k))
-    for k in reversed(range(plan.halved)):
+    for k in reversed(range(1, plan.halved)):
         held = jnp.concatenate([held, swap(held, "dp", mirror(k))])
+    beside = swap(held, "dp", mirror(0))
+    here = [over_x(plan, held), over_x(plan, beside)]
+    there = [swap(part, "col", 1) for part in here]
+    return factor(plan, where, here + there)
+
+
+def over_x(plan, part):
     for k in range(plan.xbits):
-        held = jnp.concatenate([held, swap(held, "col", 2 * mirror(k))])
-    held = jnp.concatenate([held, swap(held, "col", 1)])
-    return factor(plan, where, held)
+        part = jnp.concatenate([part, swap(part, "col", 2 * mirror(k))])
+    return part
 
 
 def solution(mesh):

time: 149 us -> 126 us (0.85)
  Pallas kernels: 57.1 us -> 48.4 us
  waiting for transfers between devices: 60.6 us -> 52.6 us
  starting transfers between devices: 22.5 us -> 19.6 us
  other arithmetic: 4.01 us -> 1.48 us
    ppermute x11 -> x15, waiting for transfers between devices: 60.6 us -> 52.6 us  [swap(): return lax.ppermute(x, axis, [(i, i ^ mask) for i in range(n)])]
    pallas_call x1, Pallas kernels: 12.4 us -> 7.9 us  [gram_pieces(): pl.pallas_call(functools.partial(gram_kernel, plan), grid_spec=pltpu.Pref...]
    ppermute x11 -> x15, starting transfers between devices: 22.5 us -> 19.6 us  [swap(): return lax.ppermute(x, axis, [(i, i ^ mask) for i in range(n)])]
    pallas_call x1, Pallas kernels: 3.47 us -> 1.14 us  [pick(): pl.pallas_call(pick_kernel, out_shape=jax.ShapeDtypeStruct((n, points.sha...]
    add x3 -> x4, other arithmetic: 2.14 us -> 0.13 us  [the longest x1 0.06 us: local(): held = kept + swap(sent, 'col', 1)]
    pallas_call x1, Pallas kernels: 41.2 us -> 39.4 us  [factor(): pl.pallas_call(functools.partial(cholesky_kernel, plan), grid_spec=pltpu....]
  transfers between devices with their start and end apart: 11 -> 15, of which waited for: 11 -> 14; matrix products, arithmetic and copies ran while one was open for 0% -> 0% of each run, Pallas kernels for 0% -> 0%
where the time goes in v2:
time: 126 us
  waiting for transfers between devices  52.6 us (42%)
  Pallas kernels  48.4 us (38%)
  starting transfers between devices  19.6 us (16%)
  local copies, waits for them, and re-layouts  3.19 us (3%)
  other arithmetic  1.48 us (1%)
    ppermute x15, waiting for transfers between devices, swap(): return lax.ppermute(x, axis, [(i, i ^ mask) for i in range(n)])  52.6 us
    pallas_call x1, Pallas kernels, factor(): pl.pallas_call(functools.partial(cholesky_kernel, plan), grid_spec=pltpu....  39.4 us
    ppermute x15, starting transfers between devices, swap(): return lax.ppermute(x, axis, [(i, i ^ mask) for i in range(n)])  19.6 us
    pallas_call x1, Pallas kernels, gram_pieces(): pl.pallas_call(functools.partial(gram_kernel, plan), grid_spec=pltpu.Pref...  7.9 us
  transfers between devices with their start and end apart: 15, of which 14 were waited for; matrix products, arithmetic and copies ran while one was open for 0% of the time, Pallas kernels for 0%

profile of v2, /device:TPU:0, one launch (start us, length us, event | category | flops | bytes accessed | tf_op | source)
XLA Modules:
  0.0 125.5 jit_solution(12021650228682053128)
XLA Ops:
  0.8 1.6 %copy-done = f32[2048,256]{1,0:T(8,128)S(1)} copy-done((f32[2048,256]{1,0:T(8,128)S(1)}, f32[2048,256]{1,0:T(8,128)}, u32[]{:S(2)}) %copy-start) | copy-done | bytes 2097176
  4.3 3.1 %collective-permute-start = (f32[128,256]{1,0:T(8,128)S(1)}, f32[128,256]{1,0:T(8,128)S(1)}, u32[]{:S(2)}, u32[]{:S(2)}) collective-permute-start(f32[128,256]{1,0:T(8,128)S(1)} %get-tuple-element.11), channel_id=1, source_target_pairs={{0,4},{4,0},{8,12},{12,8},{1,5},{5,1},{9,13},{13,9},{2,6},{6,2},{1... | collective-permute-start | bytes 393224 | tf_op jit(solution)/shard_map/ppermute | solution.py:65
  7.4 2.5 %collective-permute-start.2 = (f32[128,256]{1,0:T(8,128)S(1)}, f32[128,256]{1,0:T(8,128)S(1)}, u32[]{:S(2)}, u32[]{:S(2)}) collective-permute-start(f32[128,256]{1,0:T(8,128)S(1)} %get-tuple-element.12), channel_id=1, source_target_pairs={{0,12},{4,8},{8,4},{12,0},{1,13},{5,9},{9,5},{13,1},{2,14},{6,10},... | collective-permute-start | bytes 393224 | tf_op jit(solution)/shard_map/ppermute | solution.py:65
  10.9 5.1 %collective-permute-done.2 = f32[128,256]{1,0:T(8,128)S(1)} collective-permute-done((f32[128,256]{1,0:T(8,128)S(1)}, f32[128,256]{1,0:T(8,128)S(1)}, u32[]{:S(2)}, u32[]{:S(2)}) %collective-permute-start.2) | collective-permute-done | bytes 131104 | tf_op jit(solution)/shard_map/ppermute | solution.py:65
  16.0 1.6 %collective-permute-start.1 = (f32[128,256]{1,0:T(8,128)S(1)}, f32[128,256]{1,0:T(8,128)S(1)}, u32[]{:S(2)}, u32[]{:S(2)}) collective-permute-start(f32[128,256]{1,0:T(8,128)S(1)} %get-tuple-element.9), channel_id=1, source_target_pairs={{0,12},{4,8},{8,4},{12,0},{1,13},{5,9},{9,5},{13,1},{2,14},{6,10},... | collective-permute-start | bytes 393224 | tf_op jit(solution)/shard_map/ppermute | solution.py:65
  18.4 5.2 %collective-permute-done.1 = f32[128,256]{1,0:T(8,128)S(1)} collective-permute-done((f32[128,256]{1,0:T(8,128)S(1)}, f32[128,256]{1,0:T(8,128)S(1)}, u32[]{:S(2)}, u32[]{:S(2)}) %collective-permute-start.1) | collective-permute-done | bytes 131104 | tf_op jit(solution)/shard_map/ppermute | solution.py:65
  24.7 1.6 %collective-permute-start.4 = (f32[256,256]{1,0:T(8,128)S(1)}, f32[256,256]{1,0:T(8,128)S(1)}, u32[]{:S(2)}, u32[]{:S(2)}) collective-permute-start(f32[256,256]{1,0:T(8,128)S(1)} %pad_maximum_fusion.4), channel_id=1, source_target_pairs={{0,2},{1,3},{2,0},{3,1},{4,6},{5,7},{6,4},{7,5},{8,10},{9,11},{10,... | collective-permute-start | bytes 786440 | tf_op jit(solution)/shard_map/ppermute | solution.py:65
  26.2 6.1 %collective-permute-done.4 = f32[256,256]{1,0:T(8,128)S(1)} collective-permute-done((f32[256,256]{1,0:T(8,128)S(1)}, f32[256,256]{1,0:T(8,128)S(1)}, u32[]{:S(2)}, u32[]{:S(2)}) %collective-permute-start.4) | collective-permute-done | bytes 262176 | tf_op jit(solution)/shard_map/ppermute | solution.py:65
  32.5 1.9 %collective-permute-done.5 = f32[512,256]{1,0:T(8,128)} collective-permute-done((f32[512,256]{1,0:T(8,128)S(1)}, f32[512,256]{1,0:T(8,128)}, u32[]{:S(2)}, u32[]{:S(2)}) %collective-permute-start.5) | collective-permute-done | bytes 524320 | tf_op jit(solution)/shard_map/ppermute | solution.py:65
  35.6 7.9 %gram.1 = (f32[1152,128]{1,0:T(8,128)S(1)}, f32[1152,128]{1,0:T(8,128)S(1)}) custom-call(s32[2]{0:T(128)S(1)} %pad_add_fusion.where_ref, f32[2048,256]{1,0:T(8,128)S(1)} %copy-done.1, f32[1024,256]{1,0:T(8,128)S(1)} %pad_maximum_fusion.centers_ref), custom_call_target="tpu_custom_call" | custom-call | tf_op jit(solution)/shard_map/gram/pallas_call | solution.py:169
  43.7 1.9 %collective-permute-done.6 = f32[1152,128]{1,0:T(8,128)S(1)} collective-permute-done((f32[1152,128]{1,0:T(8,128)S(1)}, f32[1152,128]{1,0:T(8,128)S(1)}, u32[]{:S(2)}, u32[]{:S(2)}) %collective-permute-start.6) | collective-permute-done | bytes 589856 | tf_op jit(solution)/shard_map/ppermute | solution.py:65
  45.8 9.0 %collective-permute-done.7 = f32[576,128]{1,0:T(8,128)S(1)} collective-permute-done((f32[576,128]{1,0:T(8,128)S(1)}, f32[576,128]{1,0:T(8,128)S(1)}, u32[]{:S(2)}, u32[]{:S(2)}) %collective-permute-start.7) | collective-permute-done | bytes 294944 | tf_op jit(solution)/shard_map/ppermute | solution.py:65
  54.8 2.2 %collective-permute-start.8 = (f32[288,128]{1,0:T(8,128)S(1)}, f32[288,128]{1,0:T(8,128)S(1)}, u32[]{:S(2)}, u32[]{:S(2)}) collective-permute-start(f32[288,128]{1,0:T(8,128)S(1)} %slice.19), channel_id=1, source_target_pairs={{0,12},{4,8},{8,4},{12,0},{1,13},{5,9},{9,5},{13,1},{2,14},{6,10},... | collective-permute-start | bytes 442376 | tf_op jit(solution)/shard_map/ppermute | solution.py:65
  57.0 4.8 %collective-permute-done.8 = f32[288,128]{1,0:T(8,128)S(1)} collective-permute-done((f32[288,128]{1,0:T(8,128)S(1)}, f32[288,128]{1,0:T(8,128)S(1)}, u32[]{:S(2)}, u32[]{:S(2)}) %collective-permute-start.8) | collective-permute-done | bytes 147488 | tf_op jit(solution)/shard_map/ppermute | solution.py:65
  61.9 2.2 %collective-permute-start.9 = (f32[288,128]{1,0:T(8,128)S(1)}, f32[288,128]{1,0:T(8,128)S(1)}, u32[]{:S(2)}, u32[]{:S(2)}) collective-permute-start(f32[288,128]{1,0:T(8,128)S(1)} %slice_add_fusion.1), channel_id=1, source_target_pairs={{0,12},{4,8},{8,4},{12,0},{1,13},{5,9},{9,5},{13,1},{2,14},{6,10},... | collective-permute-start | bytes 442376 | tf_op jit(solution)/shard_map/ppermute | solution.py:65
  64.1 4.9 %collective-permute-done.9 = f32[288,128]{1,0:T(8,128)S(1)} collective-permute-done((f32[288,128]{1,0:T(8,128)S(1)}, f32[288,128]{1,0:T(8,128)S(1)}, u32[]{:S(2)}, u32[]{:S(2)}) %collective-permute-start.9) | collective-permute-done | bytes 147488 | tf_op jit(solution)/shard_map/ppermute | solution.py:65
  69.0 2.1 %collective-permute-start.11 = (f32[576,128]{1,0:T(8,128)S(1)}, f32[576,128]{1,0:T(8,128)S(1)}, u32[]{:S(2)}, u32[]{:S(2)}) collective-permute-start(f32[576,128]{1,0:T(8,128)S(1)} %pad_maximum_fusion.3), channel_id=1, source_target_pairs={{0,4},{4,0},{8,12},{12,8},{1,5},{5,1},{9,13},{13,9},{2,6},{6,2},{1... | collective-permute-start | bytes 884744 | tf_op jit(solution)/shard_map/ppermute | solution.py:65
  71.1 1.5 %collective-permute-start.10 = (f32[576,128]{1,0:T(8,128)S(1)}, f32[576,128]{1,0:T(8,128)S(1)}, u32[]{:S(2)}, u32[]{:S(2)}) collective-permute-start(f32[576,128]{1,0:T(8,128)S(1)} %pad_maximum_fusion.3), channel_id=1, source_target_pairs={{0,2},{1,3},{2,0},{3,1},{4,6},{5,7},{6,4},{7,5},{8,10},{9,11},{10,... | collective-permute-start | bytes 884744 | tf_op jit(solution)/shard_map/ppermute | solution.py:65
  72.6 3.2 %collective-permute-done.11 = f32[576,128]{1,0:T(8,128)S(1)} collective-permute-done((f32[576,128]{1,0:T(8,128)S(1)}, f32[576,128]{1,0:T(8,128)S(1)}, u32[]{:S(2)}, u32[]{:S(2)}) %collective-permute-start.11) | collective-permute-done | bytes 294944 | tf_op jit(solution)/shard_map/ppermute | solution.py:65
  75.8 1.5 %collective-permute-start.12 = (f32[576,128]{1,0:T(8,128)S(1)}, f32[576,128]{1,0:T(8,128)S(1)}, u32[]{:S(2)}, u32[]{:S(2)}) collective-permute-start(f32[576,128]{1,0:T(8,128)S(1)} %collective-permute-done.11), channel_id=1, source_target_pairs={{0,2},{1,3},{2,0},{3,1},{4,6},{5,7},{6,4},{7,5},{8,10},{9,11},{10,... | collective-permute-start | bytes 884744 | tf_op jit(solution)/shard_map/ppermute | solution.py:65
  77.4 3.5 %collective-permute-done.10 = f32[576,128]{1,0:T(8,128)S(1)} collective-permute-done((f32[576,128]{1,0:T(8,128)S(1)}, f32[576,128]{1,0:T(8,128)S(1)}, u32[]{:S(2)}, u32[]{:S(2)}) %collective-permute-start.10) | collective-permute-done | bytes 294944 | tf_op jit(solution)/shard_map/ppermute | solution.py:65
  81.0 3.0 %collective-permute-done.12 = f32[576,128]{1,0:T(8,128)S(1)} collective-permute-done((f32[576,128]{1,0:T(8,128)S(1)}, f32[576,128]{1,0:T(8,128)S(1)}, u32[]{:S(2)}, u32[]{:S(2)}) %collective-permute-start.12) | collective-permute-done | bytes 294944 | tf_op jit(solution)/shard_map/ppermute | solution.py:65
  84.1 2.0 %collective-permute-done.14.there1 = f32[1152,128]{1,0:T(8,128)S(1)} collective-permute-done((f32[1152,128]{1,0:T(8,128)S(1)}, f32[1152,128]{1,0:T(8,128)S(1)}, u32[]{:S(2)}, u32[]{:S(2)}) %collective-permute-start.14) | collective-permute-done | bytes 589856 | tf_op jit(solution)/shard_map/ppermute | solution.py:65
  86.1 39.4 %factor.1 = f32[1024,256]{1,0:T(8,128)} custom-call(s32[2]{0:T(128)S(1)} %pad_add_fusion.where_ref, f32[1152,128]{1,0:T(8,128)S(1)} %pad_maximum_fusion.1.here0, f32[1152,128]{1,0:T(8,128)S(1)} %constant_dynamic-update-slice_fusion.here1, f32[1152,128]{1,0:T(8,128)S(1)} %collective-permute-done.13.there0, f32[1152,128]{1,0:T(8,128)S(1)} %collective-permute-done.14.there1), custom_call_target="tpu_custom_call" | custom-call | tf_op jit(solution)/shard_map/factor/pallas_call | solution.py:314
  (33 shorter events, 7.5 us)
Async XLA Ops:
  0.8 1.6 %copy-start = (f32[2048,256]{1,0:T(8,128)S(1)}, f32[2048,256]{1,0:T(8,128)}, u32[]{:S(2)}) copy-start(f32[2048,256]{1,0:T(8,128)} %points_ref.3) | copy-start | bytes 6291460
  2.4 0.7 copy-start.2
  4.3 6.6 %collective-permute-start = (f32[128,256]{1,0:T(8,128)S(1)}, f32[128,256]{1,0:T(8,128)S(1)}, u32[]{:S(2)}, u32[]{:S(2)}) collective-permute-start(f32[128,256]{1,0:T(8,128)S(1)} %get-tuple-element.11), channel_id=1, source_target_pairs={{0,4},{4,0},{8,12},{12,8},{1,5},{5,1},{9,13},{13,9},{2,6},{6,2},{1... | collective-permute-start | bytes 393224 | tf_op jit(solution)/shard_map/ppermute | solution.py:65
  7.4 8.6 %collective-permute-start.2 = (f32[128,256]{1,0:T(8,128)S(1)}, f32[128,256]{1,0:T(8,128)S(1)}, u32[]{:S(2)}, u32[]{:S(2)}) collective-permute-start(f32[128,256]{1,0:T(8,128)S(1)} %get-tuple-element.12), channel_id=1, source_target_pairs={{0,12},{4,8},{8,4},{12,0},{1,13},{5,9},{9,5},{13,1},{2,14},{6,10},... | collective-permute-start | bytes 393224 | tf_op jit(solution)/shard_map/ppermute | solution.py:65
  16.0 7.6 %collective-permute-start.1 = (f32[128,256]{1,0:T(8,128)S(1)}, f32[128,256]{1,0:T(8,128)S(1)}, u32[]{:S(2)}, u32[]{:S(2)}) collective-permute-start(f32[128,256]{1,0:T(8,128)S(1)} %get-tuple-element.9), channel_id=1, source_target_pairs={{0,12},{4,8},{8,4},{12,0},{1,13},{5,9},{9,5},{13,1},{2,14},{6,10},... | collective-permute-start | bytes 393224 | tf_op jit(solution)/shard_map/ppermute | solution.py:65
  17.6 7.0 %collective-permute-start.3 = (f32[128,256]{1,0:T(8,128)S(1)}, f32[128,256]{1,0:T(8,128)S(1)}, u32[]{:S(2)}, u32[]{:S(2)}) collective-permute-start(f32[128,256]{1,0:T(8,128)S(1)} %get-tuple-element.10), channel_id=1, source_target_pairs={{0,4},{4,0},{8,12},{12,8},{1,5},{5,1},{9,13},{13,9},{2,6},{6,2},{1... | collective-permute-start | bytes 393224 | tf_op jit(solution)/shard_map/ppermute | solution.py:65
  23.7 11.9 %copy-start.1 = (f32[2048,256]{1,0:T(8,128)S(1)}, f32[2048,256]{1,0:T(8,128)}, u32[]{:S(2)}) copy-start(f32[2048,256]{1,0:T(8,128)} %points_ref.3) | copy-start | bytes 6291460
  24.7 7.7 %collective-permute-start.4 = (f32[256,256]{1,0:T(8,128)S(1)}, f32[256,256]{1,0:T(8,128)S(1)}, u32[]{:S(2)}, u32[]{:S(2)}) collective-permute-start(f32[256,256]{1,0:T(8,128)S(1)} %pad_maximum_fusion.4), channel_id=1, source_target_pairs={{0,2},{1,3},{2,0},{3,1},{4,6},{5,7},{6,4},{7,5},{8,10},{9,11},{10,... | collective-permute-start | bytes 786440 | tf_op jit(solution)/shard_map/ppermute | solution.py:65
  32.4 2.1 %collective-permute-start.5 = (f32[512,256]{1,0:T(8,128)S(1)}, f32[512,256]{1,0:T(8,128)}, u32[]{:S(2)}, u32[]{:S(2)}) collective-permute-start(f32[512,256]{1,0:T(8,128)S(1)} %pad_maximum_fusion.2), channel_id=1, source_target_pairs={{0,1},{1,0},{2,3},{3,2},{4,5},{5,4},{6,7},{7,6},{8,9},{9,8},{10,11... | collective-permute-start | bytes 1572872 | tf_op jit(solution)/shard_map/ppermute | solution.py:65
  43.5 2.1 %collective-permute-start.6 = (f32[1152,128]{1,0:T(8,128)S(1)}, f32[1152,128]{1,0:T(8,128)S(1)}, u32[]{:S(2)}, u32[]{:S(2)}) collective-permute-start(f32[1152,128]{1,0:T(8,128)S(1)} %get-tuple-element.8), channel_id=1, source_target_pairs={{0,1},{1,0},{2,3},{3,2},{4,5},{5,4},{6,7},{7,6},{8,9},{9,8},{10,11... | collective-permute-start | bytes 1769480 | tf_op jit(solution)/shard_map/ppermute | solution.py:65
  45.7 9.1 %collective-permute-start.7 = (f32[576,128]{1,0:T(8,128)S(1)}, f32[576,128]{1,0:T(8,128)S(1)}, u32[]{:S(2)}, u32[]{:S(2)}) collective-permute-start(f32[576,128]{1,0:T(8,128)S(1)} %slice.17), channel_id=1, source_target_pairs={{0,4},{4,0},{8,12},{12,8},{1,5},{5,1},{9,13},{13,9},{2,6},{6,2},{1... | collective-permute-start | bytes 884744 | tf_op jit(solution)/shard_map/ppermute | solution.py:65
  54.8 7.0 %collective-permute-start.8 = (f32[288,128]{1,0:T(8,128)S(1)}, f32[288,128]{1,0:T(8,128)S(1)}, u32[]{:S(2)}, u32[]{:S(2)}) collective-permute-start(f32[288,128]{1,0:T(8,128)S(1)} %slice.19), channel_id=1, source_target_pairs={{0,12},{4,8},{8,4},{12,0},{1,13},{5,9},{9,5},{13,1},{2,14},{6,10},... | collective-permute-start | bytes 442376 | tf_op jit(solution)/shard_map/ppermute | solution.py:65
  61.9 7.1 %collective-permute-start.9 = (f32[288,128]{1,0:T(8,128)S(1)}, f32[288,128]{1,0:T(8,128)S(1)}, u32[]{:S(2)}, u32[]{:S(2)}) collective-permute-start(f32[288,128]{1,0:T(8,128)S(1)} %slice_add_fusion.1), channel_id=1, source_target_pairs={{0,12},{4,8},{8,4},{12,0},{1,13},{5,9},{9,5},{13,1},{2,14},{6,10},... | collective-permute-start | bytes 442376 | tf_op jit(solution)/shard_map/ppermute | solution.py:65
  69.0 6.8 %collective-permute-start.11 = (f32[576,128]{1,0:T(8,128)S(1)}, f32[576,128]{1,0:T(8,128)S(1)}, u32[]{:S(2)}, u32[]{:S(2)}) collective-permute-start(f32[576,128]{1,0:T(8,128)S(1)} %pad_maximum_fusion.3), channel_id=1, source_target_pairs={{0,4},{4,0},{8,12},{12,8},{1,5},{5,1},{9,13},{13,9},{2,6},{6,2},{1... | collective-permute-start | bytes 884744 | tf_op jit(solution)/shard_map/ppermute | solution.py:65
  71.1 9.7 %collective-permute-start.10 = (f32[576,128]{1,0:T(8,128)S(1)}, f32[576,128]{1,0:T(8,128)S(1)}, u32[]{:S(2)}, u32[]{:S(2)}) collective-permute-start(f32[576,128]{1,0:T(8,128)S(1)} %pad_maximum_fusion.3), channel_id=1, source_target_pairs={{0,2},{1,3},{2,0},{3,1},{4,6},{5,7},{6,4},{7,5},{8,10},{9,11},{10,... | collective-permute-start | bytes 884744 | tf_op jit(solution)/shard_map/ppermute | solution.py:65
  75.8 8.2 %collective-permute-start.12 = (f32[576,128]{1,0:T(8,128)S(1)}, f32[576,128]{1,0:T(8,128)S(1)}, u32[]{:S(2)}, u32[]{:S(2)}) collective-permute-start(f32[576,128]{1,0:T(8,128)S(1)} %collective-permute-done.11), channel_id=1, source_target_pairs={{0,2},{1,3},{2,0},{3,1},{4,6},{5,7},{6,4},{7,5},{8,10},{9,11},{10,... | collective-permute-start | bytes 884744 | tf_op jit(solution)/shard_map/ppermute | solution.py:65
  80.9 3.2 %collective-permute-start.13 = (f32[1152,128]{1,0:T(8,128)S(1)}, f32[1152,128]{1,0:T(8,128)S(1)}, u32[]{:S(2)}, u32[]{:S(2)}) collective-permute-start(f32[1152,128]{1,0:T(8,128)S(1)} %pad_maximum_fusion.1.here0), channel_id=1, source_target_pairs={{0,1},{1,0},{2,3},{3,2},{4,5},{5,4},{6,7},{7,6},{8,9},{9,8},{10,11... | collective-permute-start | bytes 1769480 | tf_op jit(solution)/shard_map/ppermute | solution.py:65
  84.0 2.1 %collective-permute-start.14 = (f32[1152,128]{1,0:T(8,128)S(1)}, f32[1152,128]{1,0:T(8,128)S(1)}, u32[]{:S(2)}, u32[]{:S(2)}) collective-permute-start(f32[1152,128]{1,0:T(8,128)S(1)} %constant_dynamic-update-slice_fusion.here1), channel_id=1, source_target_pairs={{0,1},{1,0},{2,3},{3,2},{4,5},{5,4},{6,7},{7,6},{8,9},{9,8},{10,11... | collective-permute-start | bytes 1769480 | tf_op jit(solution)/shard_map/ppermute | solution.py:65

commit v3 on v2

--- a/solution.py
+++ b/solution.py
@@ -24,6 +24,15 @@
 
 def nt16(a, b):
     return lax.dot_general(a, b, (((1,), (1,)), ((), ())), preferred_element_type=F32)
+
+
+def six(x, other):
+    high, mid, low = split3(x)
+    return jnp.concatenate([low, mid, high, mid, high, high] if other else [high, mid, low, high, mid, high], axis=1)
+
+
+def nt6(a, b):
+    return nt16(six(a, False), six(b, True))
 
 
 def split2(x):
@@ -85,7 +94,7 @@
         self.rows = len(group_blocks(self.groups[0])) * NB
         rows = self.rows // 2
         self.halved = 0
-        while self.halved < self.zbits and rows % 16 == 0:
+        while self.halved < max(1, self.zbits - 1) and rows % 16 == 0:
             rows //= 2
             self.halved += 1
         self.piece = rows
@@ -117,26 +126,26 @@
     )(landmark_ids.reshape(n, 1), point_ids.reshape(1, -1), points)
 
 
-def gram_kernel(plan, where_ref, points_ref, centers_ref, kept_ref, sent_ref, centers, panel_high, panel_mid, tall):
+def gram_kernel(
+    plan, where_ref, points_ref, here0, here1, there0, there1, kept_ref, sent_ref, centers, panel_high, panel_mid, tall
+):
     col, me = where_ref[0], where_ref[1]
-    land_cols = LAND // plan.col
+    some = LAND // plan.col // 2
     half, dim = points_ref.shape
-    for r in range(plan.col):
-        rx, rc = r & (plan.nx - 1), r >> plan.xbits
-        x = ungray(gray(col >> 1) ^ rx, plan.xbits)
-        owner = (x << 1) | ((col & 1) ^ rc)
-        at = pl.multiple_of(owner * land_cols, land_cols)
-        centers[pl.ds(at, land_cols), :] = centers_ref[r * land_cols : (r + 1) * land_cols, :]
+    for part, centers_ref in enumerate((here0, here1, there0, there1)):
+        for rx in range(plan.nx):
+            x = ungray(gray(col >> 1) ^ rx, plan.xbits)
+            owner = (x << 1) | ((col & 1) ^ (part // 2))
+            at = pl.multiple_of((2 * owner + part % 2) * some, some)
+            centers[pl.ds(at, some), :] = centers_ref[rx * some : (rx + 1) * some, :]
     pts = points_ref[...]
     point_norms = nt(jnp.ones((8, dim), F32), pts * pts)[0:1, :]
-    high, mid, low = split3(pts)
-    right = jnp.concatenate([low, mid, high, mid, high, high], axis=1)
+    right = six(pts, True)
     for b in range(LAND // PAIR):
         block = slice(b * PAIR, (b + 1) * PAIR)
         c = centers[block, :]
         center_norms = jnp.sum(c * c, axis=1, keepdims=True)
-        high, mid, low = split3(c)
-        inner = nt16(jnp.concatenate([high, mid, low, high, mid, high], axis=1), right)
+        inner = nt16(six(c, False), right)
         distance = point_norms + center_norms - 2.0 * inner
         values = jnp.exp(distance * (-2.0 / dim))
         panel_high[block, :], panel_mid[block, :] = split2(values)
@@ -163,7 +172,7 @@
         out[q * plan.piece : (q + 1) * plan.piece, :] = tall[pl.ds(start, plan.piece), :]
 
 
-def gram_pieces(plan, where, points, centers):
+def gram_pieces(plan, where, points, halves):
     half = points.shape[0] // 2
     dim = points.shape[1]
     return pl.pallas_call(
@@ -173,8 +182,8 @@
             grid=(1,),
             in_specs=[
                 pl.BlockSpec((half, dim), lambda i, where: (where[0] & 1, 0)),
-                pl.BlockSpec(memory_space=pltpu.VMEM),
-            ],
+            ]
+            + [pl.BlockSpec(memory_space=pltpu.VMEM)] * 4,
             out_specs=[pl.BlockSpec(memory_space=pltpu.VMEM)] * 2,
             scratch_shapes=[
                 pltpu.VMEM((LAND, dim), F32),
@@ -186,7 +195,7 @@
         out_shape=[jax.ShapeDtypeStruct((plan.rows // 2, NB), F32)] * 2,
         compiler_params=pltpu.CompilerParams(vmem_limit_bytes=36 << 20),
         name="gram",
-    )(where, points, centers)
+    )(where, points, *halves)
 
 
 def lanecast(x, lane):
@@ -198,48 +207,85 @@
     return jnp.broadcast_to(x[row : row + 1, :], (8, NB))
 
 
-def eliminate(rows, s, lane, sub):
+def eliminate(rows, s, columns, near, lane, sub):
     own, lo = rows[s], 8 * s
-    columns = [lanecast(own, lo + j) for j in range(8)]
-    p = {(i, j): rowcast(columns[j], i) for j in range(8) for i in range(j + 1)}
+    p = list(columns)
     inside = (lane >= lo) & (lane < lo + 8)
     t = [jnp.where(inside, jnp.where(lane == lo + j, 1.0, 0.0), rowcast(own, j)) for j in range(8)]
-    inverse = []
-    for j in range(8):
-        inverse.append(1.0 / p[j, j])
-        for i in range(j + 1, 8):
-            m = p[j, i] * inverse[j]
-            for l in range(i, 8):
-                p[i, l] = p[i, l] - m * p[j, l]
-            t[i] = t[i] - m * t[j]
-    scaled = t[0] * lax.rsqrt(p[0, 0])
-    for j in range(1, 8):
-        scaled = jnp.where(sub == j, t[j] * lax.rsqrt(p[j, j]), scaled)
-    if s + 1 < STRIPS:
-        v = [t[j] * inverse[j] for j in range(8)]
+    last = s + 1 == STRIPS
+    if not last:
+        c = [lanecast(rows[s + 1], lo + j) for j in range(8)]
+        nearest = list(c)
+        following = [lanecast(rows[s + 1], lo + 8 + j) for j in range(8)]
+    upper, v, scaled = {}, [None] * 8, None
+    for j in range(0, 8, 2):
+        k = j + 1
+        pa, pb, pc = rowcast(p[j], j), rowcast(p[k], j), rowcast(p[k], k)
+        det = pa * pc - pb * pb
+        inv = 1.0 / det
+        gj, gk = inv * (pc * p[j] - pb * p[k]), inv * (pa * p[k] - pb * p[j])
+        for l in range(j + 2, 8):
+            upper[j, l], upper[k, l] = rowcast(gj, l), rowcast(gk, l)
+            p[l] = (p[l] - p[j] * upper[j, l]) - p[k] * upper[k, l]
+        if not last:
+            gj, gk = inv * (pc * c[j] - pb * c[k]), inv * (pa * c[k] - pb * c[j])
+            for l in range(j + 2, 8):
+                c[l] = (c[l] - c[j] * upper[j, l]) - c[k] * upper[k, l]
+            for l in range(8):
+                following[l] = (following[l] - c[j] * rowcast(gj, l)) - c[k] * rowcast(gk, l)
+        tw = pa * t[k] - pb * t[j]
+        v[j], v[k] = inv * (pc * t[j] - pb * t[k]), inv * tw
+        for i in range(j + 2, 8):
+            t[i] = (t[i] - upper[j, i] * t[j]) - upper[k, i] * t[k]
+        root = lax.rsqrt(pa)
+        first, second = t[j] * root, tw * (root * lax.rsqrt(det))
+        scaled = first if j == 0 else jnp.where(sub == j, first, scaled)
+        scaled = jnp.where(sub == k, second, scaled)
+    if last:
+        return scaled, None
+    for j in range(6, 0, -2):
+        for i in range(j):
+            v[i] = (v[i] - upper[i, j] * v[j]) - upper[i, j + 1] * v[j + 1]
+    for q in range(s + 1, near):
+        columns = nearest if q == s + 1 else [lanecast(rows[q], lo + j) for j in range(8)]
+        rest = jnp.where(inside, 0.0, rows[q])
         for j in range(7, -1, -1):
-            for i in range(j):
-                v[i] = v[i] - (p[i, j] * inverse[i]) * v[j]
-        for q in range(s + 1, STRIPS):
-            columns = [lanecast(rows[q], lo + j) for j in range(8)]
-            rest = jnp.where(inside, 0.0, rows[q])
-            for j in range(7, -1, -1):
-                rest = rest - columns[j] * v[j]
-            rows[q] = rest
-    return scaled
+            rest = rest - columns[j] * v[j]
+        rows[q] = rest
+    return scaled, following
+
+
+GROUP = 4
 
 
 def factor_inverse(block, inverse):
     lane = lax.broadcasted_iota(jnp.int32, (8, NB), 1)
     sub = lax.broadcasted_iota(jnp.int32, (8, NB), 0)
     rows = [block[8 * q : 8 * q + 8, :] for q in range(STRIPS)]
-    for s in range(STRIPS):
-        scaled = eliminate(rows, s, lane, sub)
-        inverse[8 * s : 8 * s + 8, :] = jnp.where(lane < 8 * (s + 1), scaled, 0.0)
+    columns = [lanecast(rows[0], j) for j in range(8)]
+    for g in range(STRIPS // GROUP):
+        near = min((g + 2) * GROUP, STRIPS)
+        lo, hi = 8 * GROUP * g, 8 * GROUP * (g + 1)
+        left, right = [], []
+        for s in range(g * GROUP, (g + 1) * GROUP):
+            scaled, columns = eliminate(rows, s, columns, near, lane, sub)
+            inverse[8 * s : 8 * s + 8, :] = jnp.where(lane < 8 * (s + 1), scaled, 0.0)
+            left.append(scaled)
+            right.append(jnp.where((lane >= 8 * (s + 1)) & (lane < hi), 0.0, scaled))
+        if near < STRIPS:
+            left, right = jnp.concatenate(left, axis=0), jnp.concatenate(right, axis=0)
+            update = lax.dot_general(
+                left[:, 8 * near :], right, (((0,), (0,)), ((), ())), precision=precise, preferred_element_type=F32
+            )
+            inside = (lane >= lo) & (lane < hi)
+            for q in range(near, STRIPS):
+                at = 8 * (q - near)
+                rows[q] = jnp.where(inside, 0.0, rows[q]) - update[at : at + 8, :]
 
 
 def cholesky_kernel(plan, where_ref, here0, here1, there0, there1, out_ref, tall, a, block, inv1, inv2, l21):
     col, me = where_ref[0], where_ref[1]
+    width = LAND // plan.col
     low = plan.halved - 1
     for rc, rz, pieces_ref in ((0, 0, here0), (0, 1, here1), (1, 0, there0), (1, 1, there1)):
         for r in range(plan.nx << low):
@@ -265,7 +311,7 @@
             @pl.when(k == 2 * t)
             def _():
                 if t:
-                    update = nt(a[lo:, :lo], a[lo : lo + PAIR, :lo])
+                    update = nt6(a[lo:, :lo], a[lo : lo + PAIR, :lo])
                     a[lo:, lo : lo + PAIR] = a[lo:, lo : lo + PAIR] - update
                 block[...] = a[lo : lo + NB, lo : lo + NB]
 
@@ -281,22 +327,27 @@
         for t in range(LAND // PAIR):
             lo = t * PAIR
 
-            @pl.when(k == 2 * t + 1)
+            @pl.when((k == 2 * t + 1) & (col * width // PAIR == t))
             def _():
-                left = nt(a[lo:, lo : lo + NB], inv1[...])
-                right = a[lo + NB :, lo + NB : lo + PAIR] - nt(left[NB:, :], l21[...])
-                right = nt(right, inv2[...])
-                a[lo : lo + NB, lo : lo + NB] = jnp.where(column <= row, left[:NB, :], 0.0)
-                a[lo + NB :, lo : lo + NB] = left[NB:, :]
-                a[lo + NB : lo + PAIR, lo + NB : lo + PAIR] = jnp.where(column <= row, right[:NB, :], 0.0)
+                top = slice(lo, lo + NB)
+                low = slice(lo + NB, lo + PAIR)
+                a[top, top] = jnp.where(column <= row, nt6(a[top, top], inv1[...]), 0.0)
+                a[low, top] = l21[...]
+                a[low, low] = jnp.where(column <= row, nt6(block[...], inv2[...]), 0.0)
+
+            @pl.when((k == 2 * t + 1) & (lo + PAIR < LAND))
+            def _():
+                rest = slice(lo + PAIR, LAND)
                 if lo + PAIR < LAND:
-                    a[lo + PAIR :, lo + NB : lo + PAIR] = right[NB:, :]
+                    left = nt6(a[rest, lo : lo + NB], inv1[...])
+                    right = a[rest, lo + NB : lo + PAIR] - nt6(left, l21[...])
+                    a[rest, lo : lo + NB] = left
+                    a[rest, lo + NB : lo + PAIR] = nt6(right, inv2[...])
 
         return carry
 
     lax.fori_loop(0, BLOCKS, step, 0)
 
-    width = LAND // plan.col
     out_ref[...] = jnp.zeros(out_ref.shape, F32)
     for c in range(plan.col):
 
@@ -339,15 +390,13 @@
     where = jnp.stack([col_index, plan.own_piece(col_index, dp_index)]).astype(jnp.int32)
 
     centers = pick(landmark_ids, point_ids, points)
-    first, second = jnp.split(centers, 2)
-    steps = list(range(plan.zbits))
-    for k, other in zip(steps, [1, 0] + steps[2:]):
-        first = first + swap(first, "dp", mirror(k))
-        second = second + swap(second, "dp", mirror(other))
-    centers = over_x(plan, jnp.concatenate([first, second]))
-    centers = jnp.concatenate([centers, swap(centers, "col", 1)])
-
-    kept, sent = gram_pieces(plan, where, points, centers)
+    halves = jnp.split(centers, 2)
+    for k in range(plan.zbits):
+        halves = [half + swap(half, "dp", mirror(k)) for half in halves]
+    halves = [over_x(plan, half) for half in halves]
+    halves = halves + [swap(half, "col", 1) for half in halves]
+
+    kept, sent = gram_pieces(plan, where, points, halves)
     held = kept + swap(sent, "col", 1)
     for k in range(plan.halved):
         half = held.shape[0] // 2

time: 126 us -> 115 us (0.913)
  Pallas kernels: 48.4 us -> 38.2 us
  starting transfers between devices: 19.6 us -> 26.3 us
  waiting for transfers between devices: 52.6 us -> 47.1 us
    pallas_call x1, Pallas kernels: 39.4 us -> 29.2 us  [factor(): pl.pallas_call(functools.partial(cholesky_kernel, plan), grid_spec=pltpu....]
    ppermute x15 -> x16, starting transfers between devices: 19.6 us -> 26.3 us  [swap(): return lax.ppermute(x, axis, [(i, i ^ mask) for i in range(n)])]
    ppermute x15 -> x16, waiting for transfers between devices: 52.6 us -> 47.1 us  [swap(): return lax.ppermute(x, axis, [(i, i ^ mask) for i in range(n)])]
  transfers between devices with their start and end apart: 15 -> 16, of which waited for: 14 -> 14; matrix products, arithmetic and copies ran while one was open for 0% -> 0% of each run, Pallas kernels for 0% -> 0%
where the time goes in v3:
time: 115 us
  waiting for transfers between devices  47.1 us (41%)
  Pallas kernels  38.2 us (33%)
  starting transfers between devices  26.3 us (23%)
  local copies, waits for them, and re-layouts  3.18 us (3%)
    ppermute x16, waiting for transfers between devices, swap(): return lax.ppermute(x, axis, [(i, i ^ mask) for i in range(n)])  47.1 us
    pallas_call x1, Pallas kernels, factor(): pl.pallas_call(functools.partial(cholesky_kernel, plan), grid_spec=pltpu....  29.2 us
    ppermute x16, starting transfers between devices, swap(): return lax.ppermute(x, axis, [(i, i ^ mask) for i in range(n)])  26.3 us
    pallas_call x1, Pallas kernels, gram_pieces(): pl.pallas_call(functools.partial(gram_kernel, plan), grid_spec=pltpu.Pref...  7.88 us
    unnamed x7, local copies, waits for them, and re-layouts  2.31 us
  transfers between devices with their start and end apart: 16, of which 14 were waited for; matrix products, arithmetic and copies ran while one was open for 0% of the time, Pallas kernels for 0%

profile of v3, /device:TPU:0, one launch (start us, length us, event | category | flops | bytes accessed | tf_op | source)
XLA Modules:
  0.0 115.2 jit_solution(16159004893076787445)
XLA Ops:
  0.8 1.6 %copy-done = f32[2048,256]{1,0:T(8,128)S(1)} copy-done((f32[2048,256]{1,0:T(8,128)S(1)}, f32[2048,256]{1,0:T(8,128)}, u32[]{:S(2)}) %copy-start) | copy-done | bytes 2097176
  4.3 3.1 %collective-permute-start.3 = (f32[128,256]{1,0:T(8,128)S(1)}, f32[128,256]{1,0:T(8,128)S(1)}, u32[]{:S(2)}, u32[]{:S(2)}) collective-permute-start(f32[128,256]{1,0:T(8,128)S(1)} %get-tuple-element.11), channel_id=1, source_target_pairs={{0,4},{4,0},{8,12},{12,8},{1,5},{5,1},{9,13},{13,9},{2,6},{6,2},{1... | collective-permute-start | bytes 393224 | tf_op jit(solution)/shard_map/ppermute | solution.py:74
  7.5 4.3 %collective-permute-done.3 = f32[128,256]{1,0:T(8,128)S(1)} collective-permute-done((f32[128,256]{1,0:T(8,128)S(1)}, f32[128,256]{1,0:T(8,128)S(1)}, u32[]{:S(2)}, u32[]{:S(2)}) %collective-permute-start.3) | collective-permute-done | bytes 131104 | tf_op jit(solution)/shard_map/ppermute | solution.py:74
  11.8 2.0 %collective-permute-done = f32[128,256]{1,0:T(8,128)S(1)} collective-permute-done((f32[128,256]{1,0:T(8,128)S(1)}, f32[128,256]{1,0:T(8,128)S(1)}, u32[]{:S(2)}, u32[]{:S(2)}) %collective-permute-start) | collective-permute-done | bytes 131104 | tf_op jit(solution)/shard_map/ppermute | solution.py:74
  13.8 3.8 %collective-permute-start.1 = (f32[128,256]{1,0:T(8,128)S(1)}, f32[128,256]{1,0:T(8,128)S(1)}, u32[]{:S(2)}, u32[]{:S(2)}) collective-permute-start(f32[128,256]{1,0:T(8,128)S(1)} %get-tuple-element.10), channel_id=1, source_target_pairs={{0,12},{4,8},{8,4},{12,0},{1,13},{5,9},{9,5},{13,1},{2,14},{6,10},... | collective-permute-start | bytes 393224 | tf_op jit(solution)/shard_map/ppermute | solution.py:74
  17.7 3.3 %collective-permute-done.1 = f32[128,256]{1,0:T(8,128)S(1)} collective-permute-done((f32[128,256]{1,0:T(8,128)S(1)}, f32[128,256]{1,0:T(8,128)S(1)}, u32[]{:S(2)}, u32[]{:S(2)}) %collective-permute-start.1) | collective-permute-done | bytes 131104 | tf_op jit(solution)/shard_map/ppermute | solution.py:74
  21.0 1.5 %collective-permute-start.2 = (f32[128,256]{1,0:T(8,128)S(1)}, f32[128,256]{1,0:T(8,128)S(1)}, u32[]{:S(2)}, u32[]{:S(2)}) collective-permute-start(f32[128,256]{1,0:T(8,128)S(1)} %add.22), channel_id=1, source_target_pairs={{0,2},{1,3},{2,0},{3,1},{4,6},{5,7},{6,4},{7,5},{8,10},{9,11},{10,... | collective-permute-start | bytes 393224 | tf_op jit(solution)/shard_map/ppermute | solution.py:74
  22.5 2.0 %collective-permute-done.4 = f32[128,256]{1,0:T(8,128)S(1)} collective-permute-done((f32[128,256]{1,0:T(8,128)S(1)}, f32[128,256]{1,0:T(8,128)S(1)}, u32[]{:S(2)}, u32[]{:S(2)}) %collective-permute-start.4) | collective-permute-done | bytes 131104 | tf_op jit(solution)/shard_map/ppermute | solution.py:74
  24.5 1.5 %collective-permute-start.5 = (f32[128,256]{1,0:T(8,128)S(1)}, f32[128,256]{1,0:T(8,128)S(1)}, u32[]{:S(2)}, u32[]{:S(2)}) collective-permute-start(f32[128,256]{1,0:T(8,128)S(1)} %add.24), channel_id=1, source_target_pairs={{0,2},{1,3},{2,0},{3,1},{4,6},{5,7},{6,4},{7,5},{8,10},{9,11},{10,... | collective-permute-start | bytes 393224 | tf_op jit(solution)/shard_map/ppermute | solution.py:74
  27.5 2.0 %collective-permute-done.5 = f32[128,256]{1,0:T(8,128)S(1)} collective-permute-done((f32[128,256]{1,0:T(8,128)S(1)}, f32[128,256]{1,0:T(8,128)S(1)}, u32[]{:S(2)}, u32[]{:S(2)}) %collective-permute-start.5) | collective-permute-done | bytes 131104 | tf_op jit(solution)/shard_map/ppermute | solution.py:74
  29.7 1.4 %collective-permute-done.7.there1 = f32[256,256]{1,0:T(8,128)S(1)} collective-permute-done((f32[256,256]{1,0:T(8,128)S(1)}, f32[256,256]{1,0:T(8,128)S(1)}, u32[]{:S(2)}, u32[]{:S(2)}) %collective-permute-start.7) | collective-permute-done | bytes 262176 | tf_op jit(solution)/shard_map/ppermute | solution.py:74
  31.1 7.9 %gram.1 = (f32[1152,128]{1,0:T(8,128)S(1)}, f32[1152,128]{1,0:T(8,128)S(1)}) custom-call(s32[2]{0:T(128)S(1)} %pad_add_fusion.where_ref, f32[2048,256]{1,0:T(8,128)S(1)} %copy-done.1, f32[256,256]{1,0:T(8,128)S(1)} %pad_maximum_fusion.1.here0, f32[256,256]{1,0:T(8,128)S(1)} %pad_maximum_fusion.2.here1, f32[256,256]{1,0:T(8,128)S(1)} %collective-permute-done.6.there0, ...), custom_call_target="tpu_custom_call" | custom-call | tf_op jit(solution)/shard_map/gram/pallas_call | solution.py:178
  39.2 1.9 %collective-permute-done.8 = f32[1152,128]{1,0:T(8,128)S(1)} collective-permute-done((f32[1152,128]{1,0:T(8,128)S(1)}, f32[1152,128]{1,0:T(8,128)S(1)}, u32[]{:S(2)}, u32[]{:S(2)}) %collective-permute-start.8) | collective-permute-done | bytes 589856 | tf_op jit(solution)/shard_map/ppermute | solution.py:74
  41.2 4.9 %collective-permute-start.9 = (f32[576,128]{1,0:T(8,128)S(1)}, f32[576,128]{1,0:T(8,128)S(1)}, u32[]{:S(2)}, u32[]{:S(2)}) collective-permute-start(f32[576,128]{1,0:T(8,128)S(1)} %slice.9), channel_id=1, source_target_pairs={{0,4},{4,0},{8,12},{12,8},{1,5},{5,1},{9,13},{13,9},{2,6},{6,2},{1... | collective-permute-start | bytes 884744 | tf_op jit(solution)/shard_map/ppermute | solution.py:74
  46.1 7.3 %collective-permute-done.9 = f32[576,128]{1,0:T(8,128)S(1)} collective-permute-done((f32[576,128]{1,0:T(8,128)S(1)}, f32[576,128]{1,0:T(8,128)S(1)}, u32[]{:S(2)}, u32[]{:S(2)}) %collective-permute-start.9) | collective-permute-done | bytes 294944 | tf_op jit(solution)/shard_map/ppermute | solution.py:74
  53.5 1.8 %collective-permute-start.10 = (f32[576,128]{1,0:T(8,128)S(1)}, f32[576,128]{1,0:T(8,128)S(1)}, u32[]{:S(2)}, u32[]{:S(2)}) collective-permute-start(f32[576,128]{1,0:T(8,128)S(1)} %slice_add_fusion), channel_id=1, source_target_pairs={{0,12},{4,8},{8,4},{12,0},{1,13},{5,9},{9,5},{13,1},{2,14},{6,10},... | collective-permute-start | bytes 884744 | tf_op jit(solution)/shard_map/ppermute | solution.py:74
  55.2 8.7 %collective-permute-done.10 = f32[576,128]{1,0:T(8,128)S(1)} collective-permute-done((f32[576,128]{1,0:T(8,128)S(1)}, f32[576,128]{1,0:T(8,128)S(1)}, u32[]{:S(2)}, u32[]{:S(2)}) %collective-permute-start.10) | collective-permute-done | bytes 294944 | tf_op jit(solution)/shard_map/ppermute | solution.py:74
  63.9 5.9 %collective-permute-start.12 = (f32[576,128]{1,0:T(8,128)S(1)}, f32[576,128]{1,0:T(8,128)S(1)}, u32[]{:S(2)}, u32[]{:S(2)}) collective-permute-start(f32[576,128]{1,0:T(8,128)S(1)} %add.27), channel_id=1, source_target_pairs={{0,4},{4,0},{8,12},{12,8},{1,5},{5,1},{9,13},{13,9},{2,6},{6,2},{1... | collective-permute-start | bytes 884744 | tf_op jit(solution)/shard_map/ppermute | solution.py:74
  69.9 1.5 %collective-permute-start.11 = (f32[576,128]{1,0:T(8,128)S(1)}, f32[576,128]{1,0:T(8,128)S(1)}, u32[]{:S(2)}, u32[]{:S(2)}) collective-permute-start(f32[576,128]{1,0:T(8,128)S(1)} %add.27), channel_id=1, source_target_pairs={{0,2},{1,3},{2,0},{3,1},{4,6},{5,7},{6,4},{7,5},{8,10},{9,11},{10,... | collective-permute-start | bytes 884744 | tf_op jit(solution)/shard_map/ppermute | solution.py:74
  71.4 4.8 %collective-permute-done.12 = f32[576,128]{1,0:T(8,128)S(1)} collective-permute-done((f32[576,128]{1,0:T(8,128)S(1)}, f32[576,128]{1,0:T(8,128)S(1)}, u32[]{:S(2)}, u32[]{:S(2)}) %collective-permute-start.12) | collective-permute-done | bytes 294944 | tf_op jit(solution)/shard_map/ppermute | solution.py:74
  76.2 1.5 %collective-permute-start.13 = (f32[576,128]{1,0:T(8,128)S(1)}, f32[576,128]{1,0:T(8,128)S(1)}, u32[]{:S(2)}, u32[]{:S(2)}) collective-permute-start(f32[576,128]{1,0:T(8,128)S(1)} %collective-permute-done.12), channel_id=1, source_target_pairs={{0,2},{1,3},{2,0},{3,1},{4,6},{5,7},{6,4},{7,5},{8,10},{9,11},{10,... | collective-permute-start | bytes 884744 | tf_op jit(solution)/shard_map/ppermute | solution.py:74
  78.1 5.8 %collective-permute-done.13 = f32[576,128]{1,0:T(8,128)S(1)} collective-permute-done((f32[576,128]{1,0:T(8,128)S(1)}, f32[576,128]{1,0:T(8,128)S(1)}, u32[]{:S(2)}, u32[]{:S(2)}) %collective-permute-start.13) | collective-permute-done | bytes 294944 | tf_op jit(solution)/shard_map/ppermute | solution.py:74
  84.1 2.0 %collective-permute-done.15.there1 = f32[1152,128]{1,0:T(8,128)S(1)} collective-permute-done((f32[1152,128]{1,0:T(8,128)S(1)}, f32[1152,128]{1,0:T(8,128)S(1)}, u32[]{:S(2)}, u32[]{:S(2)}) %collective-permute-start.15) | collective-permute-done | bytes 589856 | tf_op jit(solution)/shard_map/ppermute | solution.py:74
  86.0 29.2 %factor.1 = f32[1024,256]{1,0:T(8,128)} custom-call(s32[2]{0:T(128)S(1)} %pad_add_fusion.where_ref, f32[1152,128]{1,0:T(8,128)S(1)} %pad_maximum_fusion.here0, f32[1152,128]{1,0:T(8,128)S(1)} %constant_dynamic-update-slice_fusion.here1, f32[1152,128]{1,0:T(8,128)S(1)} %collective-permute-done.14.there0, f32[1152,128]{1,0:T(8,128)S(1)} %collective-permute-done.15.there1), custom_call_target="tpu_custom_call" | custom-call | tf_op jit(solution)/shard_map/factor/pallas_call | solution.py:365
  (32 shorter events, 5.4 us)
Async XLA Ops:
  0.8 1.6 %copy-start = (f32[2048,256]{1,0:T(8,128)S(1)}, f32[2048,256]{1,0:T(8,128)}, u32[]{:S(2)}) copy-start(f32[2048,256]{1,0:T(8,128)} %points_ref.3) | copy-start | bytes 6291460
  2.4 0.7 copy-start.2
  4.3 26.9 %copy-start.1 = (f32[2048,256]{1,0:T(8,128)S(1)}, f32[2048,256]{1,0:T(8,128)}, u32[]{:S(2)}) copy-start(f32[2048,256]{1,0:T(8,128)} %points_ref.3) | copy-start | bytes 6291460
  4.3 7.5 %collective-permute-start.3 = (f32[128,256]{1,0:T(8,128)S(1)}, f32[128,256]{1,0:T(8,128)S(1)}, u32[]{:S(2)}, u32[]{:S(2)}) collective-permute-start(f32[128,256]{1,0:T(8,128)S(1)} %get-tuple-element.11), channel_id=1, source_target_pairs={{0,4},{4,0},{8,12},{12,8},{1,5},{5,1},{9,13},{13,9},{2,6},{6,2},{1... | collective-permute-start | bytes 393224 | tf_op jit(solution)/shard_map/ppermute | solution.py:74
  7.4 6.3 %collective-permute-start = (f32[128,256]{1,0:T(8,128)S(1)}, f32[128,256]{1,0:T(8,128)S(1)}, u32[]{:S(2)}, u32[]{:S(2)}) collective-permute-start(f32[128,256]{1,0:T(8,128)S(1)} %get-tuple-element.12), channel_id=1, source_target_pairs={{0,4},{4,0},{8,12},{12,8},{1,5},{5,1},{9,13},{13,9},{2,6},{6,2},{1... | collective-permute-start | bytes 393224 | tf_op jit(solution)/shard_map/ppermute | solution.py:74
  13.8 7.2 %collective-permute-start.1 = (f32[128,256]{1,0:T(8,128)S(1)}, f32[128,256]{1,0:T(8,128)S(1)}, u32[]{:S(2)}, u32[]{:S(2)}) collective-permute-start(f32[128,256]{1,0:T(8,128)S(1)} %get-tuple-element.10), channel_id=1, source_target_pairs={{0,12},{4,8},{8,4},{12,0},{1,13},{5,9},{9,5},{13,1},{2,14},{6,10},... | collective-permute-start | bytes 393224 | tf_op jit(solution)/shard_map/ppermute | solution.py:74
  17.6 6.9 %collective-permute-start.4 = (f32[128,256]{1,0:T(8,128)S(1)}, f32[128,256]{1,0:T(8,128)S(1)}, u32[]{:S(2)}, u32[]{:S(2)}) collective-permute-start(f32[128,256]{1,0:T(8,128)S(1)} %get-tuple-element.9), channel_id=1, source_target_pairs={{0,12},{4,8},{8,4},{12,0},{1,13},{5,9},{9,5},{13,1},{2,14},{6,10},... | collective-permute-start | bytes 393224 | tf_op jit(solution)/shard_map/ppermute | solution.py:74
  21.0 6.4 %collective-permute-start.2 = (f32[128,256]{1,0:T(8,128)S(1)}, f32[128,256]{1,0:T(8,128)S(1)}, u32[]{:S(2)}, u32[]{:S(2)}) collective-permute-start(f32[128,256]{1,0:T(8,128)S(1)} %add.22), channel_id=1, source_target_pairs={{0,2},{1,3},{2,0},{3,1},{4,6},{5,7},{6,4},{7,5},{8,10},{9,11},{10,... | collective-permute-start | bytes 393224 | tf_op jit(solution)/shard_map/ppermute | solution.py:74
  24.5 5.0 %collective-permute-start.5 = (f32[128,256]{1,0:T(8,128)S(1)}, f32[128,256]{1,0:T(8,128)S(1)}, u32[]{:S(2)}, u32[]{:S(2)}) collective-permute-start(f32[128,256]{1,0:T(8,128)S(1)} %add.24), channel_id=1, source_target_pairs={{0,2},{1,3},{2,0},{3,1},{4,6},{5,7},{6,4},{7,5},{8,10},{9,11},{10,... | collective-permute-start | bytes 393224 | tf_op jit(solution)/shard_map/ppermute | solution.py:74
  27.4 2.3 %collective-permute-start.6 = (f32[256,256]{1,0:T(8,128)S(1)}, f32[256,256]{1,0:T(8,128)S(1)}, u32[]{:S(2)}, u32[]{:S(2)}) collective-permute-start(f32[256,256]{1,0:T(8,128)S(1)} %pad_maximum_fusion.1.here0), channel_id=1, source_target_pairs={{0,1},{1,0},{2,3},{3,2},{4,5},{5,4},{6,7},{7,6},{8,9},{9,8},{10,11... | collective-permute-start | bytes 786440 | tf_op jit(solution)/shard_map/ppermute | solution.py:74
  29.5 1.6 %collective-permute-start.7 = (f32[256,256]{1,0:T(8,128)S(1)}, f32[256,256]{1,0:T(8,128)S(1)}, u32[]{:S(2)}, u32[]{:S(2)}) collective-permute-start(f32[256,256]{1,0:T(8,128)S(1)} %pad_maximum_fusion.2.here1), channel_id=1, source_target_pairs={{0,1},{1,0},{2,3},{3,2},{4,5},{5,4},{6,7},{7,6},{8,9},{9,8},{10,11... | collective-permute-start | bytes 786440 | tf_op jit(solution)/shard_map/ppermute | solution.py:74
  39.0 2.1 %collective-permute-start.8 = (f32[1152,128]{1,0:T(8,128)S(1)}, f32[1152,128]{1,0:T(8,128)S(1)}, u32[]{:S(2)}, u32[]{:S(2)}) collective-permute-start(f32[1152,128]{1,0:T(8,128)S(1)} %get-tuple-element.8), channel_id=1, source_target_pairs={{0,1},{1,0},{2,3},{3,2},{4,5},{5,4},{6,7},{7,6},{8,9},{9,8},{10,11... | collective-permute-start | bytes 1769480 | tf_op jit(solution)/shard_map/ppermute | solution.py:74
  41.2 12.2 %collective-permute-start.9 = (f32[576,128]{1,0:T(8,128)S(1)}, f32[576,128]{1,0:T(8,128)S(1)}, u32[]{:S(2)}, u32[]{:S(2)}) collective-permute-start(f32[576,128]{1,0:T(8,128)S(1)} %slice.9), channel_id=1, source_target_pairs={{0,4},{4,0},{8,12},{12,8},{1,5},{5,1},{9,13},{13,9},{2,6},{6,2},{1... | collective-permute-start | bytes 884744 | tf_op jit(solution)/shard_map/ppermute | solution.py:74
  53.5 10.4 %collective-permute-start.10 = (f32[576,128]{1,0:T(8,128)S(1)}, f32[576,128]{1,0:T(8,128)S(1)}, u32[]{:S(2)}, u32[]{:S(2)}) collective-permute-start(f32[576,128]{1,0:T(8,128)S(1)} %slice_add_fusion), channel_id=1, source_target_pairs={{0,12},{4,8},{8,4},{12,0},{1,13},{5,9},{9,5},{13,1},{2,14},{6,10},... | collective-permute-start | bytes 884744 | tf_op jit(solution)/shard_map/ppermute | solution.py:74
  63.9 12.2 %collective-permute-start.12 = (f32[576,128]{1,0:T(8,128)S(1)}, f32[576,128]{1,0:T(8,128)S(1)}, u32[]{:S(2)}, u32[]{:S(2)}) collective-permute-start(f32[576,128]{1,0:T(8,128)S(1)} %add.27), channel_id=1, source_target_pairs={{0,4},{4,0},{8,12},{12,8},{1,5},{5,1},{9,13},{13,9},{2,6},{6,2},{1... | collective-permute-start | bytes 884744 | tf_op jit(solution)/shard_map/ppermute | solution.py:74
  69.9 8.1 %collective-permute-start.11 = (f32[576,128]{1,0:T(8,128)S(1)}, f32[576,128]{1,0:T(8,128)S(1)}, u32[]{:S(2)}, u32[]{:S(2)}) collective-permute-start(f32[576,128]{1,0:T(8,128)S(1)} %add.27), channel_id=1, source_target_pairs={{0,2},{1,3},{2,0},{3,1},{4,6},{5,7},{6,4},{7,5},{8,10},{9,11},{10,... | collective-permute-start | bytes 884744 | tf_op jit(solution)/shard_map/ppermute | solution.py:74
  76.2 7.8 %collective-permute-start.13 = (f32[576,128]{1,0:T(8,128)S(1)}, f32[576,128]{1,0:T(8,128)S(1)}, u32[]{:S(2)}, u32[]{:S(2)}) collective-permute-start(f32[576,128]{1,0:T(8,128)S(1)} %collective-permute-done.12), channel_id=1, source_target_pairs={{0,2},{1,3},{2,0},{3,1},{4,6},{5,7},{6,4},{7,5},{8,10},{9,11},{10,... | collective-permute-start | bytes 884744 | tf_op jit(solution)/shard_map/ppermute | solution.py:74
  78.0 6.1 %collective-permute-start.14 = (f32[1152,128]{1,0:T(8,128)S(1)}, f32[1152,128]{1,0:T(8,128)S(1)}, u32[]{:S(2)}, u32[]{:S(2)}) collective-permute-start(f32[1152,128]{1,0:T(8,128)S(1)} %pad_maximum_fusion.here0), channel_id=1, source_target_pairs={{0,1},{1,0},{2,3},{3,2},{4,5},{5,4},{6,7},{7,6},{8,9},{9,8},{10,11... | collective-permute-start | bytes 1769480 | tf_op jit(solution)/shard_map/ppermute | solution.py:74
  84.0 2.1 %collective-permute-start.15 = (f32[1152,128]{1,0:T(8,128)S(1)}, f32[1152,128]{1,0:T(8,128)S(1)}, u32[]{:S(2)}, u32[]{:S(2)}) collective-permute-start(f32[1152,128]{1,0:T(8,128)S(1)} %constant_dynamic-update-slice_fusion.here1), channel_id=1, source_target_pairs={{0,1},{1,0},{2,3},{3,2},{4,5},{5,4},{6,7},{7,6},{8,9},{9,8},{10,11... | collective-permute-start | bytes 1769480 | tf_op jit(solution)/shard_map/ppermute | solution.py:74

commit v4 on v3

--- a/solution.py
+++ b/solution.py
@@ -12,6 +12,7 @@
 PAIR = 2 * NB
 STRIPS = NB // 8
 BLOCKS = LAND // NB
+CHUNKS = 2
 
 F32 = jnp.float32
 BF16 = jnp.bfloat16
@@ -92,7 +93,7 @@
         self.xbits, self.zbits = log2(self.nx), log2(dp)
         self.groups = column_groups(self.nx)
         self.rows = len(group_blocks(self.groups[0])) * NB
-        rows = self.rows // 2
+        rows = self.rows // CHUNKS // 2
         self.halved = 0
         while self.halved < max(1, self.zbits - 1) and rows % 16 == 0:
             rows //= 2
@@ -109,7 +110,11 @@
 
 
 def pick_kernel(lid_ref, pid_ref, points_ref, out_ref):
-    matches = jnp.where(lid_ref[...] == pid_ref[...], 1.0, 0.0).astype(BF16)
+    n = lid_ref.shape[1]
+    goes_first = (gray(lax.axis_index("dp")) & 1) == 1
+    ids = jnp.broadcast_to(lid_ref[...].astype(F32), (8, n))
+    ids = jnp.where(goes_first, pltpu.roll(ids, n // 2, 1), ids)
+    matches = jnp.where(ids.T[:, 0:1] == pid_ref[...].astype(F32), 1.0, 0.0).astype(BF16)
     high, mid, low = split3(points_ref[...])
     dot = functools.partial(jnp.dot, preferred_element_type=F32)
     out_ref[...] = (dot(matches, high) + dot(matches, mid)) + dot(matches, low)
@@ -123,20 +128,22 @@
         out_specs=pl.BlockSpec(memory_space=pltpu.VMEM),
         compiler_params=pltpu.CompilerParams(vmem_limit_bytes=36 << 20),
         name="pick",
-    )(landmark_ids.reshape(n, 1), point_ids.reshape(1, -1), points)
-
-
-def gram_kernel(
-    plan, where_ref, points_ref, here0, here1, there0, there1, kept_ref, sent_ref, centers, panel_high, panel_mid, tall
-):
-    col, me = where_ref[0], where_ref[1]
+    )(landmark_ids.reshape(1, n), point_ids.reshape(1, -1), points)
+
+
+def gram_kernel(plan, where_ref, points_ref, *refs):
+    parts, refs = refs[:4], refs[4:]
+    outs = refs[: 2 * CHUNKS]
+    centers, panel_high, panel_mid, tall = refs[2 * CHUNKS :]
+    col, me, first = where_ref[0], where_ref[1], where_ref[2]
     some = LAND // plan.col // 2
-    half, dim = points_ref.shape
-    for part, centers_ref in enumerate((here0, here1, there0, there1)):
+    dim = points_ref.shape[1]
+    for n, centers_ref in enumerate(parts):
+        rc, rz = n // 2, n % 2
         for rx in range(plan.nx):
             x = ungray(gray(col >> 1) ^ rx, plan.xbits)
-            owner = (x << 1) | ((col & 1) ^ (part // 2))
-            at = pl.multiple_of((2 * owner + part % 2) * some, some)
+            owner = (x << 1) | ((col & 1) ^ rc)
+            at = pl.multiple_of((owner * 2 + (first ^ rz)) * some, some)
             centers[pl.ds(at, some), :] = centers_ref[rx * some : (rx + 1) * some, :]
     pts = points_ref[...]
     point_norms = nt(jnp.ones((8, dim), F32), pts * pts)[0:1, :]
@@ -166,13 +173,14 @@
                     tall[at : at + rows, :] = product[k * NB :, k * NB : (k + 1) * NB]
                     at += rows
 
-    for r in range(plan.pieces):
-        start = pl.multiple_of((me ^ r) * plan.piece, 8)
-        out, q = (kept_ref, r) if r < plan.pieces // 2 else (sent_ref, r - plan.pieces // 2)
-        out[q * plan.piece : (q + 1) * plan.piece, :] = tall[pl.ds(start, plan.piece), :]
-
-
-def gram_pieces(plan, where, points, halves):
+    for chunk in range(CHUNKS):
+        for r in range(plan.pieces):
+            start = pl.multiple_of((chunk * plan.pieces + (me ^ r)) * plan.piece, 8)
+            side, q = divmod(r, plan.pieces // 2)
+            outs[2 * chunk + side][q * plan.piece : (q + 1) * plan.piece, :] = tall[pl.ds(start, plan.piece), :]
+
+
+def gram_pieces(plan, where, points, parts):
     half = points.shape[0] // 2
     dim = points.shape[1]
     return pl.pallas_call(
@@ -184,7 +192,7 @@
                 pl.BlockSpec((half, dim), lambda i, where: (where[0] & 1, 0)),
             ]
             + [pl.BlockSpec(memory_space=pltpu.VMEM)] * 4,
-            out_specs=[pl.BlockSpec(memory_space=pltpu.VMEM)] * 2,
+            out_specs=[pl.BlockSpec(memory_space=pltpu.VMEM)] * (2 * CHUNKS),
             scratch_shapes=[
                 pltpu.VMEM((LAND, dim), F32),
                 pltpu.VMEM((LAND, half), BF16),
@@ -192,10 +200,10 @@
                 pltpu.VMEM((plan.rows, NB), F32),
             ],
         ),
-        out_shape=[jax.ShapeDtypeStruct((plan.rows // 2, NB), F32)] * 2,
+        out_shape=[jax.ShapeDtypeStruct((plan.rows // (2 * CHUNKS), NB), F32)] * (2 * CHUNKS),
         compiler_params=pltpu.CompilerParams(vmem_limit_bytes=36 << 20),
         name="gram",
-    )(where, points, *halves)
+    )(where, points, *parts)
 
 
 def lanecast(x, lane):
@@ -283,15 +291,18 @@
                 rows[q] = jnp.where(inside, 0.0, rows[q]) - update[at : at + 8, :]
 
 
-def cholesky_kernel(plan, where_ref, here0, here1, there0, there1, out_ref, tall, a, block, inv1, inv2, l21):
+def cholesky_kernel(plan, where_ref, *refs):
+    parts = refs[: 4 * CHUNKS]
+    out_ref, tall, a, block, inv1, inv2, l21 = refs[4 * CHUNKS :]
     col, me = where_ref[0], where_ref[1]
     width = LAND // plan.col
     low = plan.halved - 1
-    for rc, rz, pieces_ref in ((0, 0, here0), (0, 1, here1), (1, 0, there0), (1, 1, there1)):
+    for n, pieces_ref in enumerate(parts):
+        rc, chunk, rz = n // (2 * CHUNKS), n // 2 % CHUNKS, n % 2
         for r in range(plan.nx << low):
             x = ungray(gray(col >> 1) ^ (r >> low), plan.xbits)
             piece = me ^ ((rc << plan.halved) | (rz << low) | (r & ((1 << low) - 1)))
-            start = pl.multiple_of(x * plan.rows + piece * plan.piece, 8)
+            start = pl.multiple_of(x * plan.rows + (chunk * plan.pieces + piece) * plan.piece, 8)
             tall[pl.ds(start, plan.piece), :] = pieces_ref[r * plan.piece : (r + 1) * plan.piece, :]
     at = 0
     for group in plan.groups:
@@ -367,7 +378,7 @@
         grid_spec=pltpu.PrefetchScalarGridSpec(
             num_scalar_prefetch=1,
             grid=(1,),
-            in_specs=[pl.BlockSpec(memory_space=pltpu.VMEM)] * 4,
+            in_specs=[pl.BlockSpec(memory_space=pltpu.VMEM)] * (4 * CHUNKS),
             out_specs=pl.BlockSpec((LAND, width), lambda i, where: (0, 0)),
             scratch_shapes=[
                 pltpu.VMEM((total, NB), F32),
@@ -387,28 +398,31 @@
 def local(points, point_ids, landmark_ids):
     plan = Plan(lax.axis_size("dp"), lax.axis_size("col"))
     col_index, dp_index = lax.axis_index("col"), lax.axis_index("dp")
-    where = jnp.stack([col_index, plan.own_piece(col_index, dp_index)]).astype(jnp.int32)
-
-    centers = pick(landmark_ids, point_ids, points)
-    halves = jnp.split(centers, 2)
-    for k in range(plan.zbits):
-        halves = [half + swap(half, "dp", mirror(k)) for half in halves]
-    halves = [over_x(plan, half) for half in halves]
-    halves = halves + [swap(half, "col", 1) for half in halves]
-
-    kept, sent = gram_pieces(plan, where, points, halves)
-    held = kept + swap(sent, "col", 1)
+    bit = gray(dp_index) & 1
+    where = jnp.stack([col_index, plan.own_piece(col_index, dp_index), bit]).astype(jnp.int32)
+
+    held = [half_over_dp(pick(landmark_ids, point_ids, points), 0)]
+    for k in range(1, plan.zbits):
+        held = [part + swap(part, "dp", mirror(k)) for part in held]
+    here = [over_x(plan, side) for part in held for side in (part, swap(part, "dp", mirror(0)))]
+    there = [swap(part, "col", 1) for part in here]
+
+    sums = gram_pieces(plan, where, points, here + there)
+    held = [kept + swap(sent, "col", 1) for kept, sent in zip(sums[::2], sums[1::2])]
     for k in range(plan.halved):
-        half = held.shape[0] // 2
-        held = held[:half] + swap(held[half:], "dp", mirror(k))
+        held = [half_over_dp(part, k) for part in held]
     for k in range(plan.halved, plan.zbits):
-        held = held + swap(held, "dp", mirror(k))
+        held = [part + swap(part, "dp", mirror(k)) for part in held]
     for k in reversed(range(1, plan.halved)):
-        held = jnp.concatenate([held, swap(held, "dp", mirror(k))])
-    beside = swap(held, "dp", mirror(0))
-    here = [over_x(plan, held), over_x(plan, beside)]
+        held = [jnp.concatenate([part, swap(part, "dp", mirror(k))]) for part in held]
+    here = [over_x(plan, side) for part in held for side in (part, swap(part, "dp", mirror(0)))]
     there = [swap(part, "col", 1) for part in here]
     return factor(plan, where, here + there)
+
+
+def half_over_dp(part, k):
+    half = part.shape[0] // 2
+    return part[:half] + swap(part[half:], "dp", mirror(k))
 
 
 def over_x(plan, part):

time: 115 us -> 107 us (0.930)
  waiting for transfers between devices: 47.1 us -> 33.1 us
  starting transfers between devices: 26.3 us -> 31.1 us
    ppermute x16 -> x23, waiting for transfers between devices: 47.1 us -> 33.1 us  [swap(): return lax.ppermute(x, axis, [(i, i ^ mask) for i in range(n)])]
    ppermute x16 -> x23, starting transfers between devices: 26.3 us -> 31.1 us  [swap(): return lax.ppermute(x, axis, [(i, i ^ mask) for i in range(n)])]
    unnamed x7 -> x11, local copies, waits for them, and re-layouts: 2.31 us -> 3 us
  transfers between devices with their start and end apart: 16 -> 23, of which waited for: 14 -> 15; matrix products, arithmetic and copies ran while one was open for 0% -> 0% of each run, Pallas kernels for 0% -> 0%
where the time goes in v4:
time: 107 us; the launch traced here: 106 us
  Pallas kernels  38.3 us (36%)
  waiting for transfers between devices  33.1 us (31%)
  starting transfers between devices  31.1 us (29%)
  local copies, waits for them, and re-layouts  3.07 us (3%)
    ppermute x23, waiting for transfers between devices, swap(): return lax.ppermute(x, axis, [(i, i ^ mask) for i in range(n)])  33.1 us
    ppermute x23, starting transfers between devices, swap(): return lax.ppermute(x, axis, [(i, i ^ mask) for i in range(n)])  31.1 us
    pallas_call x1, Pallas kernels, factor(): pl.pallas_call(functools.partial(cholesky_kernel, plan), grid_spec=pltpu....  29.2 us
    pallas_call x1, Pallas kernels, gram_pieces(): pl.pallas_call(functools.partial(gram_kernel, plan), grid_spec=pltpu.Pref...  7.88 us
    unnamed x11, local copies, waits for them, and re-layouts  3 us
  transfers between devices with their start and end apart: 23, of which 15 were waited for; matrix products, arithmetic and copies ran while one was open for 0% of the time, Pallas kernels for 0%

profile of v4, /device:TPU:0, one launch (start us, length us, event | category | flops | bytes accessed | tf_op | source)
XLA Modules:
  0.0 106.1 jit_solution(6612523370824856247)
XLA Ops:
  0.0 1.6 %copy-done = f32[2048,256]{1,0:T(8,128)S(1)} copy-done((f32[2048,256]{1,0:T(8,128)S(1)}, f32[2048,256]{1,0:T(8,128)}, u32[]{:S(2)}) %copy-start) | copy-done | bytes 2097176
  4.3 3.1 %collective-permute-start = (f32[128,256]{1,0:T(8,128)S(1)}, f32[128,256]{1,0:T(8,128)S(1)}, u32[]{:S(2)}, u32[]{:S(2)}) collective-permute-start(f32[128,256]{1,0:T(8,128)S(1)} %slice.25), channel_id=1, source_target_pairs={{0,4},{4,0},{8,12},{12,8},{1,5},{5,1},{9,13},{13,9},{2,6},{6,2},{1... | collective-permute-start | bytes 393224 | tf_op jit(solution)/shard_map/ppermute | solution.py:75
  7.4 3.5 %collective-permute-done = f32[128,256]{1,0:T(8,128)S(1)} collective-permute-done((f32[128,256]{1,0:T(8,128)S(1)}, f32[128,256]{1,0:T(8,128)S(1)}, u32[]{:S(2)}, u32[]{:S(2)}) %collective-permute-start) | collective-permute-done | bytes 131104 | tf_op jit(solution)/shard_map/ppermute | solution.py:75
  10.9 3.8 %collective-permute-start.1 = (f32[128,256]{1,0:T(8,128)S(1)}, f32[128,256]{1,0:T(8,128)S(1)}, u32[]{:S(2)}, u32[]{:S(2)}) collective-permute-start(f32[128,256]{1,0:T(8,128)S(1)} %slice_add_fusion.2), channel_id=1, source_target_pairs={{0,12},{4,8},{8,4},{12,0},{1,13},{5,9},{9,5},{13,1},{2,14},{6,10},... | collective-permute-start | bytes 393224 | tf_op jit(solution)/shard_map/ppermute | solution.py:75
  14.7 3.0 %collective-permute-done.1 = f32[128,256]{1,0:T(8,128)S(1)} collective-permute-done((f32[128,256]{1,0:T(8,128)S(1)}, f32[128,256]{1,0:T(8,128)S(1)}, u32[]{:S(2)}, u32[]{:S(2)}) %collective-permute-start.1) | collective-permute-done | bytes 131104 | tf_op jit(solution)/shard_map/ppermute | solution.py:75
  17.8 2.2 %collective-permute-start.3 = (f32[128,256]{1,0:T(8,128)S(1)}, f32[128,256]{1,0:T(8,128)S(1)}, u32[]{:S(2)}, u32[]{:S(2)}) collective-permute-start(f32[128,256]{1,0:T(8,128)S(1)} %add.25), channel_id=1, source_target_pairs={{0,4},{4,0},{8,12},{12,8},{1,5},{5,1},{9,13},{13,9},{2,6},{6,2},{1... | collective-permute-start | bytes 393224 | tf_op jit(solution)/shard_map/ppermute | solution.py:75
  20.0 1.5 %collective-permute-start.2 = (f32[128,256]{1,0:T(8,128)S(1)}, f32[128,256]{1,0:T(8,128)S(1)}, u32[]{:S(2)}, u32[]{:S(2)}) collective-permute-start(f32[128,256]{1,0:T(8,128)S(1)} %add.25), channel_id=1, source_target_pairs={{0,2},{1,3},{2,0},{3,1},{4,6},{5,7},{6,4},{7,5},{8,10},{9,11},{10,... | collective-permute-start | bytes 393224 | tf_op jit(solution)/shard_map/ppermute | solution.py:75
  22.9 1.5 %collective-permute-start.4 = (f32[128,256]{1,0:T(8,128)S(1)}, f32[128,256]{1,0:T(8,128)S(1)}, u32[]{:S(2)}, u32[]{:S(2)}) collective-permute-start(f32[128,256]{1,0:T(8,128)S(1)} %collective-permute-done.3), channel_id=1, source_target_pairs={{0,2},{1,3},{2,0},{3,1},{4,6},{5,7},{6,4},{7,5},{8,10},{9,11},{10,... | collective-permute-start | bytes 393224 | tf_op jit(solution)/shard_map/ppermute | solution.py:75
  24.5 1.7 %collective-permute-done.2 = f32[128,256]{1,0:T(8,128)S(1)} collective-permute-done((f32[128,256]{1,0:T(8,128)S(1)}, f32[128,256]{1,0:T(8,128)S(1)}, u32[]{:S(2)}, u32[]{:S(2)}) %collective-permute-start.2) | collective-permute-done | bytes 131104 | tf_op jit(solution)/shard_map/ppermute | solution.py:75
  26.3 1.6 %collective-permute-done.4 = f32[128,256]{1,0:T(8,128)S(1)} collective-permute-done((f32[128,256]{1,0:T(8,128)S(1)}, f32[128,256]{1,0:T(8,128)S(1)}, u32[]{:S(2)}, u32[]{:S(2)}) %collective-permute-start.4) | collective-permute-done | bytes 131104 | tf_op jit(solution)/shard_map/ppermute | solution.py:75
  29.5 7.9 %gram.1 = (f32[576,128]{1,0:T(8,128)S(1)}, f32[576,128]{1,0:T(8,128)S(1)}, f32[576,128]{1,0:T(8,128)S(1)}, f32[576,128]{1,0:T(8,128)S(1)}) custom-call(s32[3]{0:T(128)S(1)} %pad_add_fusion.where_ref, f32[2048,256]{1,0:T(8,128)S(1)} %copy-done.1, f32[256,256]{1,0:T(8,128)S(1)} %pad_maximum_fusion.2.refs_0_, ...), custom_call_target="tpu_custom_call" | custom-call | tf_op jit(solution)/shard_map/gram/pallas_call | solution.py:186
  39.1 2.1 %collective-permute-start.8 = (f32[288,128]{1,0:T(8,128)S(1)}, f32[288,128]{1,0:T(8,128)S(1)}, u32[]{:S(2)}, u32[]{:S(2)}) collective-permute-start(f32[288,128]{1,0:T(8,128)S(1)} %slice.27), channel_id=1, source_target_pairs={{0,4},{4,0},{8,12},{12,8},{1,5},{5,1},{9,13},{13,9},{2,6},{6,2},{1... | collective-permute-start | bytes 442376 | tf_op jit(solution)/shard_map/ppermute | solution.py:75
  41.6 4.3 %collective-permute-done.8 = f32[288,128]{1,0:T(8,128)S(1)} collective-permute-done((f32[288,128]{1,0:T(8,128)S(1)}, f32[288,128]{1,0:T(8,128)S(1)}, u32[]{:S(2)}, u32[]{:S(2)}) %collective-permute-start.8) | collective-permute-done | bytes 147488 | tf_op jit(solution)/shard_map/ppermute | solution.py:75
  45.9 3.8 %collective-permute-start.9 = (f32[288,128]{1,0:T(8,128)S(1)}, f32[288,128]{1,0:T(8,128)S(1)}, u32[]{:S(2)}, u32[]{:S(2)}) collective-permute-start(f32[288,128]{1,0:T(8,128)S(1)} %slice_add_fusion.1), channel_id=1, source_target_pairs={{0,12},{4,8},{8,4},{12,0},{1,13},{5,9},{9,5},{13,1},{2,14},{6,10},... | collective-permute-start | bytes 442376 | tf_op jit(solution)/shard_map/ppermute | solution.py:75
  49.7 2.3 %collective-permute-start.15 = (f32[288,128]{1,0:T(8,128)S(1)}, f32[288,128]{1,0:T(8,128)S(1)}, u32[]{:S(2)}, u32[]{:S(2)}) collective-permute-start(f32[288,128]{1,0:T(8,128)S(1)} %slice_add_fusion), channel_id=1, source_target_pairs={{0,12},{4,8},{8,4},{12,0},{1,13},{5,9},{9,5},{13,1},{2,14},{6,10},... | collective-permute-start | bytes 442376 | tf_op jit(solution)/shard_map/ppermute | solution.py:75
  52.0 3.3 %collective-permute-done.9 = f32[288,128]{1,0:T(8,128)S(1)} collective-permute-done((f32[288,128]{1,0:T(8,128)S(1)}, f32[288,128]{1,0:T(8,128)S(1)}, u32[]{:S(2)}, u32[]{:S(2)}) %collective-permute-start.9) | collective-permute-done | bytes 147488 | tf_op jit(solution)/shard_map/ppermute | solution.py:75
  55.3 1.6 %collective-permute-start.10 = (f32[288,128]{1,0:T(8,128)S(1)}, f32[288,128]{1,0:T(8,128)S(1)}, u32[]{:S(2)}, u32[]{:S(2)}) collective-permute-start(f32[288,128]{1,0:T(8,128)S(1)} %add.28), channel_id=1, source_target_pairs={{0,2},{1,3},{2,0},{3,1},{4,6},{5,7},{6,4},{7,5},{8,10},{9,11},{10,... | collective-permute-start | bytes 442376 | tf_op jit(solution)/shard_map/ppermute | solution.py:75
  57.6 1.6 %collective-permute-start.16 = (f32[288,128]{1,0:T(8,128)S(1)}, f32[288,128]{1,0:T(8,128)S(1)}, u32[]{:S(2)}, u32[]{:S(2)}) collective-permute-start(f32[288,128]{1,0:T(8,128)S(1)} %add.31), channel_id=1, source_target_pairs={{0,2},{1,3},{2,0},{3,1},{4,6},{5,7},{6,4},{7,5},{8,10},{9,11},{10,... | collective-permute-start | bytes 442376 | tf_op jit(solution)/shard_map/ppermute | solution.py:75
  59.2 4.7 %collective-permute-start.11 = (f32[288,128]{1,0:T(8,128)S(1)}, f32[288,128]{1,0:T(8,128)S(1)}, u32[]{:S(2)}, u32[]{:S(2)}) collective-permute-start(f32[288,128]{1,0:T(8,128)S(1)} %add.28), channel_id=1, source_target_pairs={{0,4},{4,0},{8,12},{12,8},{1,5},{5,1},{9,13},{13,9},{2,6},{6,2},{1... | collective-permute-start | bytes 442376 | tf_op jit(solution)/shard_map/ppermute | solution.py:75
  64.7 3.6 %collective-permute-done.11 = f32[288,128]{1,0:T(8,128)S(1)} collective-permute-done((f32[288,128]{1,0:T(8,128)S(1)}, f32[288,128]{1,0:T(8,128)S(1)}, u32[]{:S(2)}, u32[]{:S(2)}) %collective-permute-start.11) | collective-permute-done | bytes 147488 | tf_op jit(solution)/shard_map/ppermute | solution.py:75
  70.4 3.3 %collective-permute-done.12 = f32[288,128]{1,0:T(8,128)S(1)} collective-permute-done((f32[288,128]{1,0:T(8,128)S(1)}, f32[288,128]{1,0:T(8,128)S(1)}, u32[]{:S(2)}, u32[]{:S(2)}) %collective-permute-start.12) | collective-permute-done | bytes 147488 | tf_op jit(solution)/shard_map/ppermute | solution.py:75
  73.8 1.5 %collective-permute-done.18 = f32[288,128]{1,0:T(8,128)S(1)} collective-permute-done((f32[288,128]{1,0:T(8,128)S(1)}, f32[288,128]{1,0:T(8,128)S(1)}, u32[]{:S(2)}, u32[]{:S(2)}) %collective-permute-start.18) | collective-permute-done | bytes 147488 | tf_op jit(solution)/shard_map/ppermute | solution.py:75
  75.4 1.5 %collective-permute-done.22.refs_7_ = f32[576,128]{1,0:T(8,128)S(1)} collective-permute-done((f32[576,128]{1,0:T(8,128)S(1)}, f32[576,128]{1,0:T(8,128)S(1)}, u32[]{:S(2)}, u32[]{:S(2)}) %collective-permute-start.22) | collective-permute-done | bytes 294944 | tf_op jit(solution)/shard_map/ppermute | solution.py:75
  77.0 29.2 %factor.1 = f32[1024,256]{1,0:T(8,128)} custom-call(s32[3]{0:T(128)S(1)} %pad_add_fusion.where_ref, f32[576,128]{1,0:T(8,128)S(1)} %pad_maximum_fusion.refs_0_, f32[576,128]{1,0:T(8,128)S(1)} %constant_dynamic-update-slice_fusion.2.refs_1_, f32[576,128]{1,0:T(8,128)S(1)} %pad_maximum_fusion.1.refs_2_, ...), custom_call_target="tpu_custom_call" | custom-call | tf_op jit(solution)/shard_map/factor/pallas_call | solution.py:376
  (54 shorter events, 11.7 us)
Async XLA Ops:
  3.0 26.6 %copy-start.1 = (f32[2048,256]{1,0:T(8,128)S(1)}, f32[2048,256]{1,0:T(8,128)}, u32[]{:S(2)}) copy-start(f32[2048,256]{1,0:T(8,128)} %points_ref.3) | copy-start | bytes 6291460
  4.3 6.6 %collective-permute-start = (f32[128,256]{1,0:T(8,128)S(1)}, f32[128,256]{1,0:T(8,128)S(1)}, u32[]{:S(2)}, u32[]{:S(2)}) collective-permute-start(f32[128,256]{1,0:T(8,128)S(1)} %slice.25), channel_id=1, source_target_pairs={{0,4},{4,0},{8,12},{12,8},{1,5},{5,1},{9,13},{13,9},{2,6},{6,2},{1... | collective-permute-start | bytes 393224 | tf_op jit(solution)/shard_map/ppermute | solution.py:75
  10.9 6.8 %collective-permute-start.1 = (f32[128,256]{1,0:T(8,128)S(1)}, f32[128,256]{1,0:T(8,128)S(1)}, u32[]{:S(2)}, u32[]{:S(2)}) collective-permute-start(f32[128,256]{1,0:T(8,128)S(1)} %slice_add_fusion.2), channel_id=1, source_target_pairs={{0,12},{4,8},{8,4},{12,0},{1,13},{5,9},{9,5},{13,1},{2,14},{6,10},... | collective-permute-start | bytes 393224 | tf_op jit(solution)/shard_map/ppermute | solution.py:75
  17.8 5.2 %collective-permute-start.3 = (f32[128,256]{1,0:T(8,128)S(1)}, f32[128,256]{1,0:T(8,128)S(1)}, u32[]{:S(2)}, u32[]{:S(2)}) collective-permute-start(f32[128,256]{1,0:T(8,128)S(1)} %add.25), channel_id=1, source_target_pairs={{0,4},{4,0},{8,12},{12,8},{1,5},{5,1},{9,13},{13,9},{2,6},{6,2},{1... | collective-permute-start | bytes 393224 | tf_op jit(solution)/shard_map/ppermute | solution.py:75
  20.0 6.1 %collective-permute-start.2 = (f32[128,256]{1,0:T(8,128)S(1)}, f32[128,256]{1,0:T(8,128)S(1)}, u32[]{:S(2)}, u32[]{:S(2)}) collective-permute-start(f32[128,256]{1,0:T(8,128)S(1)} %add.25), channel_id=1, source_target_pairs={{0,2},{1,3},{2,0},{3,1},{4,6},{5,7},{6,4},{7,5},{8,10},{9,11},{10,... | collective-permute-start | bytes 393224 | tf_op jit(solution)/shard_map/ppermute | solution.py:75
  22.9 5.0 %collective-permute-start.4 = (f32[128,256]{1,0:T(8,128)S(1)}, f32[128,256]{1,0:T(8,128)S(1)}, u32[]{:S(2)}, u32[]{:S(2)}) collective-permute-start(f32[128,256]{1,0:T(8,128)S(1)} %collective-permute-done.3), channel_id=1, source_target_pairs={{0,2},{1,3},{2,0},{3,1},{4,6},{5,7},{6,4},{7,5},{8,10},{9,11},{10,... | collective-permute-start | bytes 393224 | tf_op jit(solution)/shard_map/ppermute | solution.py:75
  26.2 1.9 %collective-permute-start.5 = (f32[256,256]{1,0:T(8,128)S(1)}, f32[256,256]{1,0:T(8,128)S(1)}, u32[]{:S(2)}, u32[]{:S(2)}) collective-permute-start(f32[256,256]{1,0:T(8,128)S(1)} %pad_maximum_fusion.2.refs_0_), channel_id=1, source_target_pairs={{0,1},{1,0},{2,3},{3,2},{4,5},{5,4},{6,7},{7,6},{8,9},{9,8},{10,11... | collective-permute-start | bytes 786440 | tf_op jit(solution)/shard_map/ppermute | solution.py:75
  27.9 1.6 %collective-permute-start.6 = (f32[256,256]{1,0:T(8,128)S(1)}, f32[256,256]{1,0:T(8,128)S(1)}, u32[]{:S(2)}, u32[]{:S(2)}) collective-permute-start(f32[256,256]{1,0:T(8,128)S(1)} %constant_dynamic-update-slice_fusion.refs_1_), channel_id=1, source_target_pairs={{0,1},{1,0},{2,3},{3,2},{4,5},{5,4},{6,7},{7,6},{8,9},{9,8},{10,11... | collective-permute-start | bytes 786440 | tf_op jit(solution)/shard_map/ppermute | solution.py:75
  37.4 1.6 %collective-permute-start.7 = (f32[576,128]{1,0:T(8,128)S(1)}, f32[576,128]{1,0:T(8,128)S(1)}, u32[]{:S(2)}, u32[]{:S(2)}) collective-permute-start(f32[576,128]{1,0:T(8,128)S(1)} %get-tuple-element.10), channel_id=1, source_target_pairs={{0,1},{1,0},{2,3},{3,2},{4,5},{5,4},{6,7},{7,6},{8,9},{9,8},{10,11... | collective-permute-start | bytes 884744 | tf_op jit(solution)/shard_map/ppermute | solution.py:75
  37.6 3.6 %collective-permute-start.13 = (f32[576,128]{1,0:T(8,128)S(1)}, f32[576,128]{1,0:T(8,128)S(1)}, u32[]{:S(2)}, u32[]{:S(2)}) collective-permute-start(f32[576,128]{1,0:T(8,128)S(1)} %get-tuple-element.12), channel_id=1, source_target_pairs={{0,1},{1,0},{2,3},{3,2},{4,5},{5,4},{6,7},{7,6},{8,9},{9,8},{10,11... | collective-permute-start | bytes 884744 | tf_op jit(solution)/shard_map/ppermute | solution.py:75
  39.1 6.8 %collective-permute-start.8 = (f32[288,128]{1,0:T(8,128)S(1)}, f32[288,128]{1,0:T(8,128)S(1)}, u32[]{:S(2)}, u32[]{:S(2)}) collective-permute-start(f32[288,128]{1,0:T(8,128)S(1)} %slice.27), channel_id=1, source_target_pairs={{0,4},{4,0},{8,12},{12,8},{1,5},{5,1},{9,13},{13,9},{2,6},{6,2},{1... | collective-permute-start | bytes 442376 | tf_op jit(solution)/shard_map/ppermute | solution.py:75
  41.3 8.4 %collective-permute-start.14 = (f32[288,128]{1,0:T(8,128)S(1)}, f32[288,128]{1,0:T(8,128)S(1)}, u32[]{:S(2)}, u32[]{:S(2)}) collective-permute-start(f32[288,128]{1,0:T(8,128)S(1)} %slice.29), channel_id=1, source_target_pairs={{0,4},{4,0},{8,12},{12,8},{1,5},{5,1},{9,13},{13,9},{2,6},{6,2},{1... | collective-permute-start | bytes 442376 | tf_op jit(solution)/shard_map/ppermute | solution.py:75
  45.9 9.4 %collective-permute-start.9 = (f32[288,128]{1,0:T(8,128)S(1)}, f32[288,128]{1,0:T(8,128)S(1)}, u32[]{:S(2)}, u32[]{:S(2)}) collective-permute-start(f32[288,128]{1,0:T(8,128)S(1)} %slice_add_fusion.1), channel_id=1, source_target_pairs={{0,12},{4,8},{8,4},{12,0},{1,13},{5,9},{9,5},{13,1},{2,14},{6,10},... | collective-permute-start | bytes 442376 | tf_op jit(solution)/shard_map/ppermute | solution.py:75
  49.7 7.9 %collective-permute-start.15 = (f32[288,128]{1,0:T(8,128)S(1)}, f32[288,128]{1,0:T(8,128)S(1)}, u32[]{:S(2)}, u32[]{:S(2)}) collective-permute-start(f32[288,128]{1,0:T(8,128)S(1)} %slice_add_fusion), channel_id=1, source_target_pairs={{0,12},{4,8},{8,4},{12,0},{1,13},{5,9},{9,5},{13,1},{2,14},{6,10},... | collective-permute-start | bytes 442376 | tf_op jit(solution)/shard_map/ppermute | solution.py:75
  55.3 8.7 %collective-permute-start.10 = (f32[288,128]{1,0:T(8,128)S(1)}, f32[288,128]{1,0:T(8,128)S(1)}, u32[]{:S(2)}, u32[]{:S(2)}) collective-permute-start(f32[288,128]{1,0:T(8,128)S(1)} %add.28), channel_id=1, source_target_pairs={{0,2},{1,3},{2,0},{3,1},{4,6},{5,7},{6,4},{7,5},{8,10},{9,11},{10,... | collective-permute-start | bytes 442376 | tf_op jit(solution)/shard_map/ppermute | solution.py:75
  57.6 6.4 %collective-permute-start.16 = (f32[288,128]{1,0:T(8,128)S(1)}, f32[288,128]{1,0:T(8,128)S(1)}, u32[]{:S(2)}, u32[]{:S(2)}) collective-permute-start(f32[288,128]{1,0:T(8,128)S(1)} %add.31), channel_id=1, source_target_pairs={{0,2},{1,3},{2,0},{3,1},{4,6},{5,7},{6,4},{7,5},{8,10},{9,11},{10,... | collective-permute-start | bytes 442376 | tf_op jit(solution)/shard_map/ppermute | solution.py:75
  59.2 9.0 %collective-permute-start.11 = (f32[288,128]{1,0:T(8,128)S(1)}, f32[288,128]{1,0:T(8,128)S(1)}, u32[]{:S(2)}, u32[]{:S(2)}) collective-permute-start(f32[288,128]{1,0:T(8,128)S(1)} %add.28), channel_id=1, source_target_pairs={{0,4},{4,0},{8,12},{12,8},{1,5},{5,1},{9,13},{13,9},{2,6},{6,2},{1... | collective-permute-start | bytes 442376 | tf_op jit(solution)/shard_map/ppermute | solution.py:75
  63.9 5.9 %collective-permute-start.17 = (f32[288,128]{1,0:T(8,128)S(1)}, f32[288,128]{1,0:T(8,128)S(1)}, u32[]{:S(2)}, u32[]{:S(2)}) collective-permute-start(f32[288,128]{1,0:T(8,128)S(1)} %add.31), channel_id=1, source_target_pairs={{0,4},{4,0},{8,12},{12,8},{1,5},{5,1},{9,13},{13,9},{2,6},{6,2},{1... | collective-permute-start | bytes 442376 | tf_op jit(solution)/shard_map/ppermute | solution.py:75
  64.0 11.4 %collective-permute-start.19 = (f32[576,128]{1,0:T(8,128)S(1)}, f32[576,128]{1,0:T(8,128)S(1)}, u32[]{:S(2)}, u32[]{:S(2)}) collective-permute-start(f32[576,128]{1,0:T(8,128)S(1)} %pad_maximum_fusion.refs_0_), channel_id=1, source_target_pairs={{0,1},{1,0},{2,3},{3,2},{4,5},{5,4},{6,7},{7,6},{8,9},{9,8},{10,11... | collective-permute-start | bytes 884744 | tf_op jit(solution)/shard_map/ppermute | solution.py:75
  64.1 11.3 %collective-permute-start.21 = (f32[576,128]{1,0:T(8,128)S(1)}, f32[576,128]{1,0:T(8,128)S(1)}, u32[]{:S(2)}, u32[]{:S(2)}) collective-permute-start(f32[576,128]{1,0:T(8,128)S(1)} %pad_maximum_fusion.1.refs_2_), channel_id=1, source_target_pairs={{0,1},{1,0},{2,3},{3,2},{4,5},{5,4},{6,7},{7,6},{8,9},{9,8},{10,11... | collective-permute-start | bytes 884744 | tf_op jit(solution)/shard_map/ppermute | solution.py:75
  68.3 5.5 %collective-permute-start.12 = (f32[288,128]{1,0:T(8,128)S(1)}, f32[288,128]{1,0:T(8,128)S(1)}, u32[]{:S(2)}, u32[]{:S(2)}) collective-permute-start(f32[288,128]{1,0:T(8,128)S(1)} %collective-permute-done.11), channel_id=1, source_target_pairs={{0,2},{1,3},{2,0},{3,1},{4,6},{5,7},{6,4},{7,5},{8,10},{9,11},{10,... | collective-permute-start | bytes 442376 | tf_op jit(solution)/shard_map/ppermute | solution.py:75
  69.8 5.5 %collective-permute-start.18 = (f32[288,128]{1,0:T(8,128)S(1)}, f32[288,128]{1,0:T(8,128)S(1)}, u32[]{:S(2)}, u32[]{:S(2)}) collective-permute-start(f32[288,128]{1,0:T(8,128)S(1)} %collective-permute-done.17), channel_id=1, source_target_pairs={{0,2},{1,3},{2,0},{3,1},{4,6},{5,7},{6,4},{7,5},{8,10},{9,11},{10,... | collective-permute-start | bytes 442376 | tf_op jit(solution)/shard_map/ppermute | solution.py:75
  73.7 1.7 %collective-permute-start.20 = (f32[576,128]{1,0:T(8,128)S(1)}, f32[576,128]{1,0:T(8,128)S(1)}, u32[]{:S(2)}, u32[]{:S(2)}) collective-permute-start(f32[576,128]{1,0:T(8,128)S(1)} %constant_dynamic-update-slice_fusion.2.refs_1_), channel_id=1, source_target_pairs={{0,1},{1,0},{2,3},{3,2},{4,5},{5,4},{6,7},{7,6},{8,9},{9,8},{10,11... | collective-permute-start | bytes 884744 | tf_op jit(solution)/shard_map/ppermute | solution.py:75
  75.3 1.6 %collective-permute-start.22 = (f32[576,128]{1,0:T(8,128)S(1)}, f32[576,128]{1,0:T(8,128)S(1)}, u32[]{:S(2)}, u32[]{:S(2)}) collective-permute-start(f32[576,128]{1,0:T(8,128)S(1)} %constant_dynamic-update-slice_fusion.4.refs_3_), channel_id=1, source_target_pairs={{0,1},{1,0},{2,3},{3,2},{4,5},{5,4},{6,7},{7,6},{8,9},{9,8},{10,11... | collective-permute-start | bytes 884744 | tf_op jit(solution)/shard_map/ppermute | solution.py:75
  (3 other events, 3.0 us)

commit v5 on v4

--- a/solution.py
+++ b/solution.py
@@ -328,10 +328,10 @@
 
         @pl.when(jnp.logical_not(first))
         def _():
-            below = nt(a[pl.ds(base + NB, NB), pl.ds(base, NB)], inv2[...])
+            below = nt6(a[pl.ds(base + NB, NB), pl.ds(base, NB)], inv2[...])
             l21[...] = below
             inv1[...] = inv2[...]
-            block[...] = a[pl.ds(base + NB, NB), pl.ds(base + NB, NB)] - nt(below, below)
+            block[...] = a[pl.ds(base + NB, NB), pl.ds(base + NB, NB)] - nt6(below, below)
 
         factor_inverse(block, inv2)
 
@@ -359,13 +359,14 @@
 
     lax.fori_loop(0, BLOCKS, step, 0)
 
-    out_ref[...] = jnp.zeros(out_ref.shape, F32)
     for c in range(plan.col):
 
         @pl.when(col == c)
         def _():
             for j in range(width // NB):
                 at = c * width + j * NB
+                for i in range(at // NB + 1, BLOCKS):
+                    out_ref[i * NB : (i + 1) * NB, j * NB : (j + 1) * NB] = jnp.zeros((NB, NB), F32)
                 for i in range(at // NB + 1):
                     out_ref[i * NB : (i + 1) * NB, j * NB : (j + 1) * NB] = a[at : at + NB, i * NB : (i + 1) * NB].T
 

time: 107 us -> 106 us (level)
  no operation moved by 1% of the time
where the time goes in v5:
time: 106 us; the launch traced here: 105 us
  Pallas kernels  37.6 us (35%)
  waiting for transfers between devices  33.1 us (31%)
  starting transfers between devices  31.1 us (29%)
  local copies, waits for them, and re-layouts  3.07 us (3%)
    ppermute x23, waiting for transfers between devices, swap(): return lax.ppermute(x, axis, [(i, i ^ mask) for i in range(n)])  33.1 us
    ppermute x23, starting transfers between devices, swap(): return lax.ppermute(x, axis, [(i, i ^ mask) for i in range(n)])  31.1 us
    pallas_call x1, Pallas kernels, factor(): pl.pallas_call(functools.partial(cholesky_kernel, plan), grid_spec=pltpu....  28.5 us
    pallas_call x1, Pallas kernels, gram_pieces(): pl.pallas_call(functools.partial(gram_kernel, plan), grid_spec=pltpu.Pref...  7.88 us
    unnamed x11, local copies, waits for them, and re-layouts  3 us
  transfers between devices with their start and end apart: 23, of which 15 were waited for; matrix products, arithmetic and copies ran while one was open for 0% of the time, Pallas kernels for 0%

profile of v5, /device:TPU:0, one launch (start us, length us, event | category | flops | bytes accessed | tf_op | source)
XLA Modules:
  0.0 105.4 jit_solution(5970339521971139564)
XLA Ops:
  0.0 1.6 %copy-done = f32[2048,256]{1,0:T(8,128)S(1)} copy-done((f32[2048,256]{1,0:T(8,128)S(1)}, f32[2048,256]{1,0:T(8,128)}, u32[]{:S(2)}) %copy-start) | copy-done | bytes 2097176
  4.3 3.1 %collective-permute-start = (f32[128,256]{1,0:T(8,128)S(1)}, f32[128,256]{1,0:T(8,128)S(1)}, u32[]{:S(2)}, u32[]{:S(2)}) collective-permute-start(f32[128,256]{1,0:T(8,128)S(1)} %slice.25), channel_id=1, source_target_pairs={{0,4},{4,0},{8,12},{12,8},{1,5},{5,1},{9,13},{13,9},{2,6},{6,2},{1... | collective-permute-start | bytes 393224 | tf_op jit(solution)/shard_map/ppermute | solution.py:75
  7.4 3.5 %collective-permute-done = f32[128,256]{1,0:T(8,128)S(1)} collective-permute-done((f32[128,256]{1,0:T(8,128)S(1)}, f32[128,256]{1,0:T(8,128)S(1)}, u32[]{:S(2)}, u32[]{:S(2)}) %collective-permute-start) | collective-permute-done | bytes 131104 | tf_op jit(solution)/shard_map/ppermute | solution.py:75
  10.9 3.8 %collective-permute-start.1 = (f32[128,256]{1,0:T(8,128)S(1)}, f32[128,256]{1,0:T(8,128)S(1)}, u32[]{:S(2)}, u32[]{:S(2)}) collective-permute-start(f32[128,256]{1,0:T(8,128)S(1)} %slice_add_fusion.2), channel_id=1, source_target_pairs={{0,12},{4,8},{8,4},{12,0},{1,13},{5,9},{9,5},{13,1},{2,14},{6,10},... | collective-permute-start | bytes 393224 | tf_op jit(solution)/shard_map/ppermute | solution.py:75
  14.7 3.0 %collective-permute-done.1 = f32[128,256]{1,0:T(8,128)S(1)} collective-permute-done((f32[128,256]{1,0:T(8,128)S(1)}, f32[128,256]{1,0:T(8,128)S(1)}, u32[]{:S(2)}, u32[]{:S(2)}) %collective-permute-start.1) | collective-permute-done | bytes 131104 | tf_op jit(solution)/shard_map/ppermute | solution.py:75
  17.8 2.2 %collective-permute-start.3 = (f32[128,256]{1,0:T(8,128)S(1)}, f32[128,256]{1,0:T(8,128)S(1)}, u32[]{:S(2)}, u32[]{:S(2)}) collective-permute-start(f32[128,256]{1,0:T(8,128)S(1)} %add.25), channel_id=1, source_target_pairs={{0,4},{4,0},{8,12},{12,8},{1,5},{5,1},{9,13},{13,9},{2,6},{6,2},{1... | collective-permute-start | bytes 393224 | tf_op jit(solution)/shard_map/ppermute | solution.py:75
  20.0 1.5 %collective-permute-start.2 = (f32[128,256]{1,0:T(8,128)S(1)}, f32[128,256]{1,0:T(8,128)S(1)}, u32[]{:S(2)}, u32[]{:S(2)}) collective-permute-start(f32[128,256]{1,0:T(8,128)S(1)} %add.25), channel_id=1, source_target_pairs={{0,2},{1,3},{2,0},{3,1},{4,6},{5,7},{6,4},{7,5},{8,10},{9,11},{10,... | collective-permute-start | bytes 393224 | tf_op jit(solution)/shard_map/ppermute | solution.py:75
  22.9 1.5 %collective-permute-start.4 = (f32[128,256]{1,0:T(8,128)S(1)}, f32[128,256]{1,0:T(8,128)S(1)}, u32[]{:S(2)}, u32[]{:S(2)}) collective-permute-start(f32[128,256]{1,0:T(8,128)S(1)} %collective-permute-done.3), channel_id=1, source_target_pairs={{0,2},{1,3},{2,0},{3,1},{4,6},{5,7},{6,4},{7,5},{8,10},{9,11},{10,... | collective-permute-start | bytes 393224 | tf_op jit(solution)/shard_map/ppermute | solution.py:75
  24.5 1.7 %collective-permute-done.2 = f32[128,256]{1,0:T(8,128)S(1)} collective-permute-done((f32[128,256]{1,0:T(8,128)S(1)}, f32[128,256]{1,0:T(8,128)S(1)}, u32[]{:S(2)}, u32[]{:S(2)}) %collective-permute-start.2) | collective-permute-done | bytes 131104 | tf_op jit(solution)/shard_map/ppermute | solution.py:75
  26.3 1.6 %collective-permute-done.4 = f32[128,256]{1,0:T(8,128)S(1)} collective-permute-done((f32[128,256]{1,0:T(8,128)S(1)}, f32[128,256]{1,0:T(8,128)S(1)}, u32[]{:S(2)}, u32[]{:S(2)}) %collective-permute-start.4) | collective-permute-done | bytes 131104 | tf_op jit(solution)/shard_map/ppermute | solution.py:75
  29.5 7.9 %gram.1 = (f32[576,128]{1,0:T(8,128)S(1)}, f32[576,128]{1,0:T(8,128)S(1)}, f32[576,128]{1,0:T(8,128)S(1)}, f32[576,128]{1,0:T(8,128)S(1)}) custom-call(s32[3]{0:T(128)S(1)} %pad_add_fusion.where_ref, f32[2048,256]{1,0:T(8,128)S(1)} %copy-done.1, f32[256,256]{1,0:T(8,128)S(1)} %pad_maximum_fusion.2.refs_0_, ...), custom_call_target="tpu_custom_call" | custom-call | tf_op jit(solution)/shard_map/gram/pallas_call | solution.py:186
  39.1 2.1 %collective-permute-start.8 = (f32[288,128]{1,0:T(8,128)S(1)}, f32[288,128]{1,0:T(8,128)S(1)}, u32[]{:S(2)}, u32[]{:S(2)}) collective-permute-start(f32[288,128]{1,0:T(8,128)S(1)} %slice.27), channel_id=1, source_target_pairs={{0,4},{4,0},{8,12},{12,8},{1,5},{5,1},{9,13},{13,9},{2,6},{6,2},{1... | collective-permute-start | bytes 442376 | tf_op jit(solution)/shard_map/ppermute | solution.py:75
  41.6 4.3 %collective-permute-done.8 = f32[288,128]{1,0:T(8,128)S(1)} collective-permute-done((f32[288,128]{1,0:T(8,128)S(1)}, f32[288,128]{1,0:T(8,128)S(1)}, u32[]{:S(2)}, u32[]{:S(2)}) %collective-permute-start.8) | collective-permute-done | bytes 147488 | tf_op jit(solution)/shard_map/ppermute | solution.py:75
  45.9 3.8 %collective-permute-start.9 = (f32[288,128]{1,0:T(8,128)S(1)}, f32[288,128]{1,0:T(8,128)S(1)}, u32[]{:S(2)}, u32[]{:S(2)}) collective-permute-start(f32[288,128]{1,0:T(8,128)S(1)} %slice_add_fusion.1), channel_id=1, source_target_pairs={{0,12},{4,8},{8,4},{12,0},{1,13},{5,9},{9,5},{13,1},{2,14},{6,10},... | collective-permute-start | bytes 442376 | tf_op jit(solution)/shard_map/ppermute | solution.py:75
  49.7 2.3 %collective-permute-start.15 = (f32[288,128]{1,0:T(8,128)S(1)}, f32[288,128]{1,0:T(8,128)S(1)}, u32[]{:S(2)}, u32[]{:S(2)}) collective-permute-start(f32[288,128]{1,0:T(8,128)S(1)} %slice_add_fusion), channel_id=1, source_target_pairs={{0,12},{4,8},{8,4},{12,0},{1,13},{5,9},{9,5},{13,1},{2,14},{6,10},... | collective-permute-start | bytes 442376 | tf_op jit(solution)/shard_map/ppermute | solution.py:75
  52.0 3.3 %collective-permute-done.9 = f32[288,128]{1,0:T(8,128)S(1)} collective-permute-done((f32[288,128]{1,0:T(8,128)S(1)}, f32[288,128]{1,0:T(8,128)S(1)}, u32[]{:S(2)}, u32[]{:S(2)}) %collective-permute-start.9) | collective-permute-done | bytes 147488 | tf_op jit(solution)/shard_map/ppermute | solution.py:75
  55.3 1.6 %collective-permute-start.10 = (f32[288,128]{1,0:T(8,128)S(1)}, f32[288,128]{1,0:T(8,128)S(1)}, u32[]{:S(2)}, u32[]{:S(2)}) collective-permute-start(f32[288,128]{1,0:T(8,128)S(1)} %add.28), channel_id=1, source_target_pairs={{0,2},{1,3},{2,0},{3,1},{4,6},{5,7},{6,4},{7,5},{8,10},{9,11},{10,... | collective-permute-start | bytes 442376 | tf_op jit(solution)/shard_map/ppermute | solution.py:75
  57.6 1.6 %collective-permute-start.16 = (f32[288,128]{1,0:T(8,128)S(1)}, f32[288,128]{1,0:T(8,128)S(1)}, u32[]{:S(2)}, u32[]{:S(2)}) collective-permute-start(f32[288,128]{1,0:T(8,128)S(1)} %add.31), channel_id=1, source_target_pairs={{0,2},{1,3},{2,0},{3,1},{4,6},{5,7},{6,4},{7,5},{8,10},{9,11},{10,... | collective-permute-start | bytes 442376 | tf_op jit(solution)/shard_map/ppermute | solution.py:75
  59.2 4.7 %collective-permute-start.11 = (f32[288,128]{1,0:T(8,128)S(1)}, f32[288,128]{1,0:T(8,128)S(1)}, u32[]{:S(2)}, u32[]{:S(2)}) collective-permute-start(f32[288,128]{1,0:T(8,128)S(1)} %add.28), channel_id=1, source_target_pairs={{0,4},{4,0},{8,12},{12,8},{1,5},{5,1},{9,13},{13,9},{2,6},{6,2},{1... | collective-permute-start | bytes 442376 | tf_op jit(solution)/shard_map/ppermute | solution.py:75
  64.7 3.6 %collective-permute-done.11 = f32[288,128]{1,0:T(8,128)S(1)} collective-permute-done((f32[288,128]{1,0:T(8,128)S(1)}, f32[288,128]{1,0:T(8,128)S(1)}, u32[]{:S(2)}, u32[]{:S(2)}) %collective-permute-start.11) | collective-permute-done | bytes 147488 | tf_op jit(solution)/shard_map/ppermute | solution.py:75
  70.4 3.3 %collective-permute-done.12 = f32[288,128]{1,0:T(8,128)S(1)} collective-permute-done((f32[288,128]{1,0:T(8,128)S(1)}, f32[288,128]{1,0:T(8,128)S(1)}, u32[]{:S(2)}, u32[]{:S(2)}) %collective-permute-start.12) | collective-permute-done | bytes 147488 | tf_op jit(solution)/shard_map/ppermute | solution.py:75
  73.8 1.5 %collective-permute-done.18 = f32[288,128]{1,0:T(8,128)S(1)} collective-permute-done((f32[288,128]{1,0:T(8,128)S(1)}, f32[288,128]{1,0:T(8,128)S(1)}, u32[]{:S(2)}, u32[]{:S(2)}) %collective-permute-start.18) | collective-permute-done | bytes 147488 | tf_op jit(solution)/shard_map/ppermute | solution.py:75
  75.4 1.5 %collective-permute-done.22.refs_7_ = f32[576,128]{1,0:T(8,128)S(1)} collective-permute-done((f32[576,128]{1,0:T(8,128)S(1)}, f32[576,128]{1,0:T(8,128)S(1)}, u32[]{:S(2)}, u32[]{:S(2)}) %collective-permute-start.22) | collective-permute-done | bytes 294944 | tf_op jit(solution)/shard_map/ppermute | solution.py:75
  77.0 28.5 %factor.1 = f32[1024,256]{1,0:T(8,128)} custom-call(s32[3]{0:T(128)S(1)} %pad_add_fusion.where_ref, f32[576,128]{1,0:T(8,128)S(1)} %pad_maximum_fusion.refs_0_, f32[576,128]{1,0:T(8,128)S(1)} %constant_dynamic-update-slice_fusion.2.refs_1_, f32[576,128]{1,0:T(8,128)S(1)} %pad_maximum_fusion.1.refs_2_, ...), custom_call_target="tpu_custom_call" | custom-call | tf_op jit(solution)/shard_map/factor/pallas_call | solution.py:377
  (54 shorter events, 11.7 us)
Async XLA Ops:
  3.0 26.6 %copy-start.1 = (f32[2048,256]{1,0:T(8,128)S(1)}, f32[2048,256]{1,0:T(8,128)}, u32[]{:S(2)}) copy-start(f32[2048,256]{1,0:T(8,128)} %points_ref.3) | copy-start | bytes 6291460
  4.3 6.6 %collective-permute-start = (f32[128,256]{1,0:T(8,128)S(1)}, f32[128,256]{1,0:T(8,128)S(1)}, u32[]{:S(2)}, u32[]{:S(2)}) collective-permute-start(f32[128,256]{1,0:T(8,128)S(1)} %slice.25), channel_id=1, source_target_pairs={{0,4},{4,0},{8,12},{12,8},{1,5},{5,1},{9,13},{13,9},{2,6},{6,2},{1... | collective-permute-start | bytes 393224 | tf_op jit(solution)/shard_map/ppermute | solution.py:75
  10.9 6.8 %collective-permute-start.1 = (f32[128,256]{1,0:T(8,128)S(1)}, f32[128,256]{1,0:T(8,128)S(1)}, u32[]{:S(2)}, u32[]{:S(2)}) collective-permute-start(f32[128,256]{1,0:T(8,128)S(1)} %slice_add_fusion.2), channel_id=1, source_target_pairs={{0,12},{4,8},{8,4},{12,0},{1,13},{5,9},{9,5},{13,1},{2,14},{6,10},... | collective-permute-start | bytes 393224 | tf_op jit(solution)/shard_map/ppermute | solution.py:75
  17.8 5.2 %collective-permute-start.3 = (f32[128,256]{1,0:T(8,128)S(1)}, f32[128,256]{1,0:T(8,128)S(1)}, u32[]{:S(2)}, u32[]{:S(2)}) collective-permute-start(f32[128,256]{1,0:T(8,128)S(1)} %add.25), channel_id=1, source_target_pairs={{0,4},{4,0},{8,12},{12,8},{1,5},{5,1},{9,13},{13,9},{2,6},{6,2},{1... | collective-permute-start | bytes 393224 | tf_op jit(solution)/shard_map/ppermute | solution.py:75
  20.0 6.1 %collective-permute-start.2 = (f32[128,256]{1,0:T(8,128)S(1)}, f32[128,256]{1,0:T(8,128)S(1)}, u32[]{:S(2)}, u32[]{:S(2)}) collective-permute-start(f32[128,256]{1,0:T(8,128)S(1)} %add.25), channel_id=1, source_target_pairs={{0,2},{1,3},{2,0},{3,1},{4,6},{5,7},{6,4},{7,5},{8,10},{9,11},{10,... | collective-permute-start | bytes 393224 | tf_op jit(solution)/shard_map/ppermute | solution.py:75
  22.9 5.0 %collective-permute-start.4 = (f32[128,256]{1,0:T(8,128)S(1)}, f32[128,256]{1,0:T(8,128)S(1)}, u32[]{:S(2)}, u32[]{:S(2)}) collective-permute-start(f32[128,256]{1,0:T(8,128)S(1)} %collective-permute-done.3), channel_id=1, source_target_pairs={{0,2},{1,3},{2,0},{3,1},{4,6},{5,7},{6,4},{7,5},{8,10},{9,11},{10,... | collective-permute-start | bytes 393224 | tf_op jit(solution)/shard_map/ppermute | solution.py:75
  26.2 1.9 %collective-permute-start.5 = (f32[256,256]{1,0:T(8,128)S(1)}, f32[256,256]{1,0:T(8,128)S(1)}, u32[]{:S(2)}, u32[]{:S(2)}) collective-permute-start(f32[256,256]{1,0:T(8,128)S(1)} %pad_maximum_fusion.2.refs_0_), channel_id=1, source_target_pairs={{0,1},{1,0},{2,3},{3,2},{4,5},{5,4},{6,7},{7,6},{8,9},{9,8},{10,11... | collective-permute-start | bytes 786440 | tf_op jit(solution)/shard_map/ppermute | solution.py:75
  27.9 1.6 %collective-permute-start.6 = (f32[256,256]{1,0:T(8,128)S(1)}, f32[256,256]{1,0:T(8,128)S(1)}, u32[]{:S(2)}, u32[]{:S(2)}) collective-permute-start(f32[256,256]{1,0:T(8,128)S(1)} %constant_dynamic-update-slice_fusion.refs_1_), channel_id=1, source_target_pairs={{0,1},{1,0},{2,3},{3,2},{4,5},{5,4},{6,7},{7,6},{8,9},{9,8},{10,11... | collective-permute-start | bytes 786440 | tf_op jit(solution)/shard_map/ppermute | solution.py:75
  37.4 1.6 %collective-permute-start.7 = (f32[576,128]{1,0:T(8,128)S(1)}, f32[576,128]{1,0:T(8,128)S(1)}, u32[]{:S(2)}, u32[]{:S(2)}) collective-permute-start(f32[576,128]{1,0:T(8,128)S(1)} %get-tuple-element.10), channel_id=1, source_target_pairs={{0,1},{1,0},{2,3},{3,2},{4,5},{5,4},{6,7},{7,6},{8,9},{9,8},{10,11... | collective-permute-start | bytes 884744 | tf_op jit(solution)/shard_map/ppermute | solution.py:75
  37.6 3.6 %collective-permute-start.13 = (f32[576,128]{1,0:T(8,128)S(1)}, f32[576,128]{1,0:T(8,128)S(1)}, u32[]{:S(2)}, u32[]{:S(2)}) collective-permute-start(f32[576,128]{1,0:T(8,128)S(1)} %get-tuple-element.12), channel_id=1, source_target_pairs={{0,1},{1,0},{2,3},{3,2},{4,5},{5,4},{6,7},{7,6},{8,9},{9,8},{10,11... | collective-permute-start | bytes 884744 | tf_op jit(solution)/shard_map/ppermute | solution.py:75
  39.1 6.8 %collective-permute-start.8 = (f32[288,128]{1,0:T(8,128)S(1)}, f32[288,128]{1,0:T(8,128)S(1)}, u32[]{:S(2)}, u32[]{:S(2)}) collective-permute-start(f32[288,128]{1,0:T(8,128)S(1)} %slice.27), channel_id=1, source_target_pairs={{0,4},{4,0},{8,12},{12,8},{1,5},{5,1},{9,13},{13,9},{2,6},{6,2},{1... | collective-permute-start | bytes 442376 | tf_op jit(solution)/shard_map/ppermute | solution.py:75
  41.3 8.4 %collective-permute-start.14 = (f32[288,128]{1,0:T(8,128)S(1)}, f32[288,128]{1,0:T(8,128)S(1)}, u32[]{:S(2)}, u32[]{:S(2)}) collective-permute-start(f32[288,128]{1,0:T(8,128)S(1)} %slice.29), channel_id=1, source_target_pairs={{0,4},{4,0},{8,12},{12,8},{1,5},{5,1},{9,13},{13,9},{2,6},{6,2},{1... | collective-permute-start | bytes 442376 | tf_op jit(solution)/shard_map/ppermute | solution.py:75
  45.9 9.4 %collective-permute-start.9 = (f32[288,128]{1,0:T(8,128)S(1)}, f32[288,128]{1,0:T(8,128)S(1)}, u32[]{:S(2)}, u32[]{:S(2)}) collective-permute-start(f32[288,128]{1,0:T(8,128)S(1)} %slice_add_fusion.1), channel_id=1, source_target_pairs={{0,12},{4,8},{8,4},{12,0},{1,13},{5,9},{9,5},{13,1},{2,14},{6,10},... | collective-permute-start | bytes 442376 | tf_op jit(solution)/shard_map/ppermute | solution.py:75
  49.7 7.9 %collective-permute-start.15 = (f32[288,128]{1,0:T(8,128)S(1)}, f32[288,128]{1,0:T(8,128)S(1)}, u32[]{:S(2)}, u32[]{:S(2)}) collective-permute-start(f32[288,128]{1,0:T(8,128)S(1)} %slice_add_fusion), channel_id=1, source_target_pairs={{0,12},{4,8},{8,4},{12,0},{1,13},{5,9},{9,5},{13,1},{2,14},{6,10},... | collective-permute-start | bytes 442376 | tf_op jit(solution)/shard_map/ppermute | solution.py:75
  55.3 8.7 %collective-permute-start.10 = (f32[288,128]{1,0:T(8,128)S(1)}, f32[288,128]{1,0:T(8,128)S(1)}, u32[]{:S(2)}, u32[]{:S(2)}) collective-permute-start(f32[288,128]{1,0:T(8,128)S(1)} %add.28), channel_id=1, source_target_pairs={{0,2},{1,3},{2,0},{3,1},{4,6},{5,7},{6,4},{7,5},{8,10},{9,11},{10,... | collective-permute-start | bytes 442376 | tf_op jit(solution)/shard_map/ppermute | solution.py:75
  57.6 6.4 %collective-permute-start.16 = (f32[288,128]{1,0:T(8,128)S(1)}, f32[288,128]{1,0:T(8,128)S(1)}, u32[]{:S(2)}, u32[]{:S(2)}) collective-permute-start(f32[288,128]{1,0:T(8,128)S(1)} %add.31), channel_id=1, source_target_pairs={{0,2},{1,3},{2,0},{3,1},{4,6},{5,7},{6,4},{7,5},{8,10},{9,11},{10,... | collective-permute-start | bytes 442376 | tf_op jit(solution)/shard_map/ppermute | solution.py:75
  59.2 9.0 %collective-permute-start.11 = (f32[288,128]{1,0:T(8,128)S(1)}, f32[288,128]{1,0:T(8,128)S(1)}, u32[]{:S(2)}, u32[]{:S(2)}) collective-permute-start(f32[288,128]{1,0:T(8,128)S(1)} %add.28), channel_id=1, source_target_pairs={{0,4},{4,0},{8,12},{12,8},{1,5},{5,1},{9,13},{13,9},{2,6},{6,2},{1... | collective-permute-start | bytes 442376 | tf_op jit(solution)/shard_map/ppermute | solution.py:75
  63.9 5.9 %collective-permute-start.17 = (f32[288,128]{1,0:T(8,128)S(1)}, f32[288,128]{1,0:T(8,128)S(1)}, u32[]{:S(2)}, u32[]{:S(2)}) collective-permute-start(f32[288,128]{1,0:T(8,128)S(1)} %add.31), channel_id=1, source_target_pairs={{0,4},{4,0},{8,12},{12,8},{1,5},{5,1},{9,13},{13,9},{2,6},{6,2},{1... | collective-permute-start | bytes 442376 | tf_op jit(solution)/shard_map/ppermute | solution.py:75
  64.0 11.4 %collective-permute-start.19 = (f32[576,128]{1,0:T(8,128)S(1)}, f32[576,128]{1,0:T(8,128)S(1)}, u32[]{:S(2)}, u32[]{:S(2)}) collective-permute-start(f32[576,128]{1,0:T(8,128)S(1)} %pad_maximum_fusion.refs_0_), channel_id=1, source_target_pairs={{0,1},{1,0},{2,3},{3,2},{4,5},{5,4},{6,7},{7,6},{8,9},{9,8},{10,11... | collective-permute-start | bytes 884744 | tf_op jit(solution)/shard_map/ppermute | solution.py:75
  64.1 11.3 %collective-permute-start.21 = (f32[576,128]{1,0:T(8,128)S(1)}, f32[576,128]{1,0:T(8,128)S(1)}, u32[]{:S(2)}, u32[]{:S(2)}) collective-permute-start(f32[576,128]{1,0:T(8,128)S(1)} %pad_maximum_fusion.1.refs_2_), channel_id=1, source_target_pairs={{0,1},{1,0},{2,3},{3,2},{4,5},{5,4},{6,7},{7,6},{8,9},{9,8},{10,11... | collective-permute-start | bytes 884744 | tf_op jit(solution)/shard_map/ppermute | solution.py:75
  68.3 5.5 %collective-permute-start.12 = (f32[288,128]{1,0:T(8,128)S(1)}, f32[288,128]{1,0:T(8,128)S(1)}, u32[]{:S(2)}, u32[]{:S(2)}) collective-permute-start(f32[288,128]{1,0:T(8,128)S(1)} %collective-permute-done.11), channel_id=1, source_target_pairs={{0,2},{1,3},{2,0},{3,1},{4,6},{5,7},{6,4},{7,5},{8,10},{9,11},{10,... | collective-permute-start | bytes 442376 | tf_op jit(solution)/shard_map/ppermute | solution.py:75
  69.8 5.5 %collective-permute-start.18 = (f32[288,128]{1,0:T(8,128)S(1)}, f32[288,128]{1,0:T(8,128)S(1)}, u32[]{:S(2)}, u32[]{:S(2)}) collective-permute-start(f32[288,128]{1,0:T(8,128)S(1)} %collective-permute-done.17), channel_id=1, source_target_pairs={{0,2},{1,3},{2,0},{3,1},{4,6},{5,7},{6,4},{7,5},{8,10},{9,11},{10,... | collective-permute-start | bytes 442376 | tf_op jit(solution)/shard_map/ppermute | solution.py:75
  73.7 1.7 %collective-permute-start.20 = (f32[576,128]{1,0:T(8,128)S(1)}, f32[576,128]{1,0:T(8,128)S(1)}, u32[]{:S(2)}, u32[]{:S(2)}) collective-permute-start(f32[576,128]{1,0:T(8,128)S(1)} %constant_dynamic-update-slice_fusion.2.refs_1_), channel_id=1, source_target_pairs={{0,1},{1,0},{2,3},{3,2},{4,5},{5,4},{6,7},{7,6},{8,9},{9,8},{10,11... | collective-permute-start | bytes 884744 | tf_op jit(solution)/shard_map/ppermute | solution.py:75
  75.3 1.6 %collective-permute-start.22 = (f32[576,128]{1,0:T(8,128)S(1)}, f32[576,128]{1,0:T(8,128)S(1)}, u32[]{:S(2)}, u32[]{:S(2)}) collective-permute-start(f32[576,128]{1,0:T(8,128)S(1)} %constant_dynamic-update-slice_fusion.4.refs_3_), channel_id=1, source_target_pairs={{0,1},{1,0},{2,3},{3,2},{4,5},{5,4},{6,7},{7,6},{8,9},{9,8},{10,11... | collective-permute-start | bytes 884744 | tf_op jit(solution)/shard_map/ppermute | solution.py:75
  (3 other events, 3.0 us)
